TPU v7x, 32 devices: a whole 2x2x4 slice. The times are simulated.
32 devices in a mesh: row: 4 (over x, core), col: 8 (over z, y).
Axes of the slice: x: 2, y: 2, z: 4, core: 2. Of those that a mesh axis runs over, the one named last changes fastest.
Arguments:
- points: bfloat16 [12, 4, 512, 64], P(None, 'row', 'col'), may hold values from -7.5 to 7.5
- inverse_factor: bfloat16 [512, 512], replicated, as said below
- panel_index: int32 [1], replicated, may hold values from 3 to 23
- column_map: int32 [8], P('col'), may hold values from 0 to 7, each once
Outputs:
- panel: bfloat16 [6, 4, 512, 512], P(None, 'row', 'col')
- update: bfloat16 [6, 4, 512, 8, 512], P(None, 'row', None, 'col')
Inputs may be any that keep to these rules, and one draw needn't show every extreme that they name: `column_map`: a permutation of 0 .. 8 - 1. `inverse_factor`: zero above the diagonal.
All inputs are finite; a program needn't handle non-finite values.
Results may differ from a plain program's by a relative error of at most 0.0049.
Values may be sent and summed in bfloat16 or wider, within the bound.
No kernel may reach another device: no remote copies, remote signals or barrier semaphores. Data moves between devices by JAX's collectives and lax.ppermute only.
A program may use at most 64 MiB of HBM per device.

v0:
```python
import functools

import jax
import jax.numpy as jnp
from jax import lax
from jax.experimental import pallas as pl
from jax.experimental.pallas import tpu as pltpu
from jax.sharding import PartitionSpec as P


RW = 6
JITTER = 1.0
LANES = 128


NT = (((1,), (1,)), ((), ()))
NN = (((1,), (0,)), ((), ()))


def dot(left, right, dims):
    return lax.dot_general(left, right, dims, preferred_element_type=jnp.float32)


PIECES = 3


def pieces_of(values):
    pieces = []
    for _ in range(PIECES):
        piece = values.astype(jnp.bfloat16)
        pieces.append(piece)
        values = values - piece.astype(jnp.float32)
    return pieces


def half_norms(packed, fold, dim):
    vals = packed.astype(jnp.float32)
    squares = vals * vals
    high = squares.astype(jnp.bfloat16)
    low = (squares - high.astype(jnp.float32)).astype(jnp.bfloat16)
    width = fold * dim
    part_of_row = (lax.broadcasted_iota(jnp.int32, (2 * width, fold * LANES), 0) % width) // dim
    part_of_lane = lax.broadcasted_iota(jnp.int32, (2 * width, fold * LANES), 1) // LANES
    mask = jnp.where(part_of_row == part_of_lane, 0.5, 0.0).astype(jnp.bfloat16)
    norms = dot(jnp.concatenate([high, low], axis=1), mask, NN)
    return [norms[:, part * LANES : (part + 1) * LANES] for part in range(fold)]


def with_norms(points, norm, first, second, dim):
    rows = points.shape[0]
    lane = lax.broadcasted_iota(jnp.int32, (rows, LANES - dim), 1)
    tail = jnp.zeros((rows, LANES - dim), jnp.float32)
    for base, what in ((0, first), (PIECES, second)):
        if what is None:
            for n, piece in enumerate(pieces_of(norm[:, : LANES - dim])):
                tail = jnp.where(lane == base + n, piece.astype(jnp.float32), tail)
        else:
            tail = jnp.where((lane >= base) & (lane < base + PIECES), what, tail)
    return jnp.concatenate([points, tail.astype(jnp.bfloat16)], axis=1)


def pick_kernel(peers, scalars, *refs):
    chunks, out = refs[:peers], refs[peers]
    position = scalars[0]
    for k in range(peers):
        out[0, k] = chunks[k][0]
        out[1, k] = chunks[k][1 + position]


def prep_kernel(peers, fold, dim, *refs):
    chunks = refs[:peers]
    factor, left, factor_t = refs[peers:]
    half = chunks[0].shape[1]
    width = fold * dim
    for k in range(peers):
        packed = chunks[k][1:].reshape(RW * half, width)
        for part, norm in enumerate(half_norms(packed, fold, dim)):
            rows = with_norms(packed[:, part * dim : (part + 1) * dim], norm, None, 1.0, dim)
            left[k, :, part * half : (part + 1) * half, :] = rows.reshape(RW, half, LANES)
    factor_t[...] = factor[...].T


def main_kernel(peers, sources, fold, dim, group, scalars, *refs):
    left = refs[0]
    held = refs[1 : 1 + sources]
    factor, factor_t, panel_out, update_out = refs[1 + sources : 5 + sources]
    right_p, right_j, left_j, mat, kip, ent, obuf, sem = refs[5 + sources :]
    side = factor.shape[0]
    share = left.shape[2]
    half = share // fold
    cut = side // 2
    col_here = scalars[0]
    scale = 1.0 / dim

    for which, right in ((0, right_p), (1, right_j)):
        source = scalars[1 + which]
        blocks = []
        for k in range(peers):
            block = held[0][which, k]
            for other in range(1, sources):
                block = jnp.where(source == other, held[other][which, k], block)
            blocks.append(block)
        packed = jnp.concatenate(blocks, axis=0)
        for part, norm in enumerate(half_norms(packed, fold, dim)):
            points = packed[:, part * dim : (part + 1) * dim]
            scaled = (points.astype(jnp.float32) * scale).astype(jnp.bfloat16)
            rows = with_norms(scaled, norm * -scale, -scale, None, dim)
            lefts = with_norms(points, norm, None, 1.0, dim) if which else None
            for k in range(peers):
                start = pl.multiple_of((col_here ^ k) * share + part * half, half)
                right[pl.ds(start, half), :] = rows[k * half : (k + 1) * half]
                if which:
                    left_j[pl.ds(start, half), :] = lefts[k * half : (k + 1) * half]

    kjp = jnp.exp(dot(left_j[...], right_p[...], NT)).astype(jnp.bfloat16)

    def by_factor(values):
        return jnp.concatenate(
            [
                dot(values[:, :cut], factor[:cut, :cut], NT),
                dot(values, factor[cut:, :], NT),
            ],
            axis=1,
        ).astype(jnp.bfloat16)

    def kernels(step):
        members = left[step * group : (step + 1) * group].reshape(group * RW * share, LANES)
        slot = step % 2
        kip[slot] = jnp.exp(dot(members, right_p[...], NT)).astype(jnp.bfloat16)
        ent[slot] = jnp.exp(dot(members, right_j[...], NT))
        for m in range(group):
            row0 = (col_here ^ (step * group + m)) * share
            lane0 = pl.multiple_of((row0 // LANES) * LANES, LANES)
            at = pl.ds(pl.multiple_of((m * RW + scalars[3]) * share, share), share)
            rows = lax.broadcasted_iota(jnp.int32, (share, LANES), 0) + row0
            cols = lax.broadcasted_iota(jnp.int32, (share, LANES), 1) + lane0
            hit = (rows == cols) & (scalars[4] > 0)
            ent[slot, at, pl.ds(lane0, LANES)] += jnp.where(hit, JITTER, 0.0)

    steps = peers // group
    lcol = by_factor(kjp)
    kernels(0)
    panel_out[...] = by_factor(kip[0, : RW * share]).reshape(RW, share, side)
    mat[:cut] = dot(factor_t[:cut], lcol, NT).astype(jnp.bfloat16)
    mat[cut:] = dot(factor_t[cut:, cut:], lcol[:, cut:], NT).astype(jnp.bfloat16)

    copies = []
    for step in range(steps):
        if step + 1 < steps:
            kernels(step + 1)
        slot = step % 2
        result = (ent[slot] - dot(kip[slot], mat[...], NN)).astype(jnp.bfloat16)
        obuf[step] = result.reshape(group, RW, share, side)
        for m in range(group):
            row0 = pl.multiple_of((col_here ^ (step * group + m)) * share, share)
            copy = pltpu.make_async_copy(
                obuf.at[step, m], update_out.at[:, pl.ds(row0, share), :], sem.at[step, m]
            )
            copy.start()
            copies.append(copy)
    for copy in copies:
        copy.wait()


def step(points, inverse_factor, panel_index, column_map):
    row_count = lax.axis_size("row")
    col_count = lax.axis_size("col")
    row_here = lax.axis_index("row")
    col_here = lax.axis_index("col")
    side = inverse_factor.shape[0]
    share, dim = points.shape[2], points.shape[3]
    fold = max(1, LANES // dim)
    half = share // fold
    peers = col_count
    group = min(2, peers)
    rows = RW * share

    pivot_tile = panel_index[0]
    start_slot = (pivot_tile + row_count - row_here) // row_count
    local_points = lax.dynamic_slice_in_dim(points[:, 0], start_slot - 1, RW + 1, 0)
    packed = jnp.concatenate(
        [local_points[:, part * half : (part + 1) * half] for part in range(fold)], axis=-1
    )
    chunks = [packed] + [None] * (peers - 1)
    for k in range(1, peers):
        chunks[k] = lax.ppermute(packed, "col", [(c, c ^ k) for c in range(col_count)])

    column_tile = pivot_tile + 1 + column_map[0]
    panel_owner = pivot_tile % row_count
    column_owner = column_tile % row_count
    position = jnp.clip(column_tile // row_count - start_slot, 0, RW - 1)
    vmem = pl.BlockSpec(memory_space=pltpu.VMEM)
    smem = pl.BlockSpec(memory_space=pltpu.SMEM)
    held = pl.pallas_call(
        functools.partial(pick_kernel, peers),
        out_shape=jax.ShapeDtypeStruct((2, peers, half, fold * dim), jnp.bfloat16),
        in_specs=[smem] + [vmem] * peers,
        out_specs=vmem,
        compiler_params=pltpu.CompilerParams(vmem_limit_bytes=4 << 20),
        name="pick",
    )(position[None].astype(jnp.int32), *chunks)

    sources = {0: held}
    bit = row_count >> 1
    while bit:
        for source in sorted(sources, reverse=True):
            sources[source ^ bit] = lax.ppermute(
                sources[source], "row", [(r, r ^ bit) for r in range(row_count)]
            )
        bit >>= 1
    sources = [sources[source] for source in range(row_count)]

    diag_slot = jnp.where(column_owner == row_here, position, 0)
    scalars = jnp.stack(
        [
            col_here,
            panel_owner ^ row_here,
            column_owner ^ row_here,
            diag_slot,
            (column_owner == row_here).astype(jnp.int32),
        ]
    ).astype(jnp.int32)
    steps = peers // group
    prep = pl.pallas_call(
        functools.partial(prep_kernel, peers, fold, dim),
        out_shape=(
            jax.ShapeDtypeStruct((peers, RW, share, LANES), jnp.bfloat16),
            jax.ShapeDtypeStruct((side, side), jnp.bfloat16),
        ),
        in_specs=[vmem] * (peers + 1),
        out_specs=(vmem, vmem),
        compiler_params=pltpu.CompilerParams(vmem_limit_bytes=8 << 20),
        cost_estimate=pl.CostEstimate(
            flops=4 * peers * RW * half * LANES * LANES,
            bytes_accessed=4 * peers * rows * LANES,
            transcendentals=0,
        ),
        name="prep",
    )
    left, factor_t = prep(*chunks, inverse_factor)
    panel_part, update = pl.pallas_call(
        functools.partial(main_kernel, peers, row_count, fold, dim, group),
        out_shape=(
            jax.ShapeDtypeStruct((RW, share, side), jnp.bfloat16),
            jax.ShapeDtypeStruct((RW, side, side), jnp.bfloat16),
        ),
        in_specs=[smem] + [vmem] * (row_count + 3),
        out_specs=(vmem, pl.BlockSpec(memory_space=pl.ANY)),
        scratch_shapes=[
            pltpu.VMEM((side, LANES), jnp.bfloat16),
            pltpu.VMEM((side, LANES), jnp.bfloat16),
            pltpu.VMEM((side, LANES), jnp.bfloat16),
            pltpu.VMEM((side, side), jnp.bfloat16),
            pltpu.VMEM((2, group * rows, side), jnp.bfloat16),
            pltpu.VMEM((2, group * rows, side), jnp.float32),
            pltpu.VMEM((steps, group, RW, share, side), jnp.bfloat16),
            pltpu.SemaphoreType.DMA((steps, group)),
        ],
        compiler_params=pltpu.CompilerParams(vmem_limit_bytes=40 << 20),
        name="tiles",
    )(scalars, left, *sources, inverse_factor, factor_t)
    return panel_part[:, None], update[:, None, :, None, :]


def solution(mesh):
    in_specs = (P(None, "row", "col", None), P(), P(), P("col"))
    out_specs = (P(None, "row", "col", None), P(None, "row", None, "col", None))
    return jax.shard_map(step, mesh=mesh, in_specs=in_specs, out_specs=out_specs, check_vma=False)
```

profile of v0, /device:TPU:0, one launch (start us, length us, event | category | flops | bytes accessed | tf_op | source)
XLA Modules:
  0.0 33.3 jit_solution(6519982485863948737)
XLA Ops:
  0.6 0.0 copy-start
  1.4 0.2 copy-done
  1.6 0.1 pad_maximum_fusion.refs_0_
  1.7 6.1 %collective-permute-start.6 = (bf16[7,32,128]{2,1,0:T(8,128)(2,1)S(1)}, bf16[7,32,128]{2,1,0:T(8,128)(2,1)S(1)}, u32[]{:S(2)}, u32[]{:S(2)}) collective-permute-start(bf16[7,32,128]{2,1,0:T(8,128)(2,1)S(1)} %pad_maximum_fusion.refs_0_), channel_id=1, source_target_pairs={{0,7},{1,6},{2,5},{3,4},{4,3},{5,2},{6,1},{7,0},{8,15},{9,14},{10,... | collective-permute-start | bytes 172040 | tf_op jit(solution)/shard_map/ppermute | solution.py:186
  7.8 0.2 collective-permute-start.5
  8.0 0.7 %collective-permute-start.4 = (bf16[7,32,128]{2,1,0:T(8,128)(2,1)S(1)}, bf16[7,32,128]{2,1,0:T(8,128)(2,1)S(1)}, u32[]{:S(2)}, u32[]{:S(2)}) collective-permute-start(bf16[7,32,128]{2,1,0:T(8,128)(2,1)S(1)} %pad_maximum_fusion.refs_0_), channel_id=1, source_target_pairs={{0,5},{1,4},{2,7},{3,6},{4,1},{5,0},{6,3},{7,2},{8,13},{9,12},{10,... | collective-permute-start | bytes 172040 | tf_op jit(solution)/shard_map/ppermute | solution.py:186
  8.8 2.0 %collective-permute-start.3 = (bf16[7,32,128]{2,1,0:T(8,128)(2,1)S(1)}, bf16[7,32,128]{2,1,0:T(8,128)(2,1)S(1)}, u32[]{:S(2)}, u32[]{:S(2)}) collective-permute-start(bf16[7,32,128]{2,1,0:T(8,128)(2,1)S(1)} %pad_maximum_fusion.refs_0_), channel_id=1, source_target_pairs={{0,4},{1,5},{2,6},{3,7},{4,0},{5,1},{6,2},{7,3},{8,12},{9,13},{10,... | collective-permute-start | bytes 172040 | tf_op jit(solution)/shard_map/ppermute | solution.py:186
  10.8 2.3 %collective-permute-start.2 = (bf16[7,32,128]{2,1,0:T(8,128)(2,1)S(1)}, bf16[7,32,128]{2,1,0:T(8,128)(2,1)S(1)}, u32[]{:S(2)}, u32[]{:S(2)}) collective-permute-start(bf16[7,32,128]{2,1,0:T(8,128)(2,1)S(1)} %pad_maximum_fusion.refs_0_), channel_id=1, source_target_pairs={{0,3},{1,2},{2,1},{3,0},{4,7},{5,6},{6,5},{7,4},{8,11},{9,10},{10,... | collective-permute-start | bytes 172040 | tf_op jit(solution)/shard_map/ppermute | solution.py:186
  13.1 0.0 collective-permute-done.6.refs_7_
  13.1 0.8 %collective-permute-start.1 = (bf16[7,32,128]{2,1,0:T(8,128)(2,1)S(1)}, bf16[7,32,128]{2,1,0:T(8,128)(2,1)S(1)}, u32[]{:S(2)}, u32[]{:S(2)}) collective-permute-start(bf16[7,32,128]{2,1,0:T(8,128)(2,1)S(1)} %pad_maximum_fusion.refs_0_), channel_id=1, source_target_pairs={{0,2},{1,3},{2,0},{3,1},{4,6},{5,7},{6,4},{7,5},{8,10},{9,11},{10,... | collective-permute-start | bytes 172040 | tf_op jit(solution)/shard_map/ppermute | solution.py:186
  13.9 0.0 collective-permute-done.5.refs_6_
  13.9 0.4 %collective-permute-start = (bf16[7,32,128]{2,1,0:T(8,128)(2,1)S(1)}, bf16[7,32,128]{2,1,0:T(8,128)(2,1)S(1)}, u32[]{:S(2)}, u32[]{:S(2)}) collective-permute-start(bf16[7,32,128]{2,1,0:T(8,128)(2,1)S(1)} %pad_maximum_fusion.refs_0_), channel_id=1, source_target_pairs={{0,1},{1,0},{2,3},{3,2},{4,5},{5,4},{6,7},{7,6},{8,9},{9,8},{10,11... | collective-permute-start | bytes 172040 | tf_op jit(solution)/shard_map/ppermute | solution.py:186
  15.0 1.3 %collective-permute-done.4.refs_5_ = bf16[7,32,128]{2,1,0:T(8,128)(2,1)S(1)} collective-permute-done((bf16[7,32,128]{2,1,0:T(8,128)(2,1)S(1)}, bf16[7,32,128]{2,1,0:T(8,128)(2,1)S(1)}, u32[]{:S(2)}, u32[]{:S(2)}) %collective-permute-start.4) | collective-permute-done | bytes 57376 | tf_op jit(solution)/shard_map/ppermute | solution.py:186
  16.3 1.5 %collective-permute-done.3.refs_4_ = bf16[7,32,128]{2,1,0:T(8,128)(2,1)S(1)} collective-permute-done((bf16[7,32,128]{2,1,0:T(8,128)(2,1)S(1)}, bf16[7,32,128]{2,1,0:T(8,128)(2,1)S(1)}, u32[]{:S(2)}, u32[]{:S(2)}) %collective-permute-start.3) | collective-permute-done | bytes 57376 | tf_op jit(solution)/shard_map/ppermute | solution.py:186
  17.7 0.1 collective-permute-done.2.refs_3_
  17.8 0.4 %collective-permute-done.1.refs_2_ = bf16[7,32,128]{2,1,0:T(8,128)(2,1)S(1)} collective-permute-done((bf16[7,32,128]{2,1,0:T(8,128)(2,1)S(1)}, bf16[7,32,128]{2,1,0:T(8,128)(2,1)S(1)}, u32[]{:S(2)}, u32[]{:S(2)}) %collective-permute-start.1) | collective-permute-done | bytes 57376 | tf_op jit(solution)/shard_map/ppermute | solution.py:186
  18.3 0.0 collective-permute-done.refs_1_
  18.3 1.6 %collective-permute-start.8 = (bf16[2,8,32,128]{3,2,1,0:T(8,128)(2,1)S(1)}, bf16[2,8,32,128]{3,2,1,0:T(8,128)(2,1)S(1)}, u32[]{:S(2)}, u32[]{:S(2)}) collective-permute-start(bf16[2,8,32,128]{3,2,1,0:T(8,128)(2,1)S(1)} %pick.1.refs_1_), channel_id=1, source_target_pairs={{0,16},{8,24},{16,0},{24,8},{1,17},{9,25},{17,1},{25,9},{2,18},{10... | collective-permute-start | bytes 393224 | tf_op jit(solution)/shard_map/ppermute | solution.py:207
  19.9 0.0 collective-permute-start.7
  19.9 3.4 %collective-permute-done.8.refs_3_ = bf16[2,8,32,128]{3,2,1,0:T(8,128)(2,1)S(1)} collective-permute-done((bf16[2,8,32,128]{3,2,1,0:T(8,128)(2,1)S(1)}, bf16[2,8,32,128]{3,2,1,0:T(8,128)(2,1)S(1)}, u32[]{:S(2)}, u32[]{:S(2)}) %collective-permute-start.8) | collective-permute-done | bytes 131104 | tf_op jit(solution)/shard_map/ppermute | solution.py:207
  23.3 0.0 collective-permute-start.9
  23.3 0.1 stack.27.scalars
  23.4 0.0 copy-start.1
  23.4 1.0 %copy-done.1 = bf16[512,512]{1,0:T(8,128)(2,1)S(1)} copy-done((bf16[512,512]{1,0:T(8,128)(2,1)S(1)}, bf16[512,512]{1,0:T(8,128)(2,1)}, u32[]{:S(2)}) %copy-start.1) | copy-done | bytes 524312
  24.5 0.9 %prep.1 = (bf16[8,6,64,128]{3,2,1,0:T(8,128)(2,1)S(1)}, bf16[512,512]{1,0:T(8,128)(2,1)S(1)}) custom-call(bf16[7,32,128]{2,1,0:T(8,128)(2,1)S(1)} %pad_maximum_fusion.refs_0_, bf16[7,32,128]{2,1,0:T(8,128)(2,1)S(1)} %collective-permute-done.refs_1_, bf16[7,32,128]{2,1,0:T(8,128)(2,1)S(1)} %collective-permute-done.1.refs_2_, ...), custom_call_target="tpu_custom_call" | custom-call | flops 100663296 | bytes 1572864 | tf_op jit(solution)/shard_map/prep/pallas_call | solution.py:240
  25.4 0.0 collective-permute-done.7.refs_2_
  25.4 0.0 collective-permute-done.9.refs_4_
  25.4 0.0 copy-start.2
  25.4 1.0 %copy-done.2 = bf16[512,512]{1,0:T(8,128)(2,1)S(1)} copy-done((bf16[512,512]{1,0:T(8,128)(2,1)S(1)}, bf16[512,512]{1,0:T(8,128)(2,1)}, u32[]{:S(2)}) %copy-start.2) | copy-done | bytes 524312
  26.5 6.8 %tiles.1 = (bf16[6,64,512]{2,1,0:T(8,128)(2,1)}, bf16[6,512,512]{2,1,0:T(8,128)(2,1)}) custom-call(s32[5]{0:T(128)S(1)} %stack.27.scalars, bf16[8,6,64,128]{3,2,1,0:T(8,128)(2,1)S(1)} %get-tuple-element.6.refs_0_, bf16[2,8,32,128]{3,2,1,0:T(8,128)(2,1)S(1)} %pick.1.refs_1_, bf16[2,8,32,128]{3,2,1,0:T(8,128)(2,1)S(1)} %collective-permute-done.7.refs_2_, ...), custom_call_target="tpu_custom_call" | custom-call | tf_op jit(solution)/shard_map/tiles/pallas_call | solution.py:241
  (3 shorter events, 0.0 us)
Async XLA Ops:
  0.6 0.9 %copy-start = (bf16[12,1,64,64]{3,2,1,0:T(8,128)(2,1)S(1)}, bf16[12,1,64,64]{3,2,1,0:T(8,128)(2,1)}, u32[]{:S(2)}) copy-start(bf16[12,1,64,64]{3,2,1,0:T(8,128)(2,1)} %param.4) | copy-start | bytes 294916
  1.7 11.4 %collective-permute-start.6 = (bf16[7,32,128]{2,1,0:T(8,128)(2,1)S(1)}, bf16[7,32,128]{2,1,0:T(8,128)(2,1)S(1)}, u32[]{:S(2)}, u32[]{:S(2)}) collective-permute-start(bf16[7,32,128]{2,1,0:T(8,128)(2,1)S(1)} %pad_maximum_fusion.refs_0_), channel_id=1, source_target_pairs={{0,7},{1,6},{2,5},{3,4},{4,3},{5,2},{6,1},{7,0},{8,15},{9,14},{10,... | collective-permute-start | bytes 172040 | tf_op jit(solution)/shard_map/ppermute | solution.py:186
  7.8 6.1 %collective-permute-start.5 = (bf16[7,32,128]{2,1,0:T(8,128)(2,1)S(1)}, bf16[7,32,128]{2,1,0:T(8,128)(2,1)S(1)}, u32[]{:S(2)}, u32[]{:S(2)}) collective-permute-start(bf16[7,32,128]{2,1,0:T(8,128)(2,1)S(1)} %pad_maximum_fusion.refs_0_), channel_id=1, source_target_pairs={{0,6},{1,7},{2,4},{3,5},{4,2},{5,3},{6,0},{7,1},{8,14},{9,15},{10,... | collective-permute-start | bytes 172040 | tf_op jit(solution)/shard_map/ppermute | solution.py:186
  8.0 8.2 %collective-permute-start.4 = (bf16[7,32,128]{2,1,0:T(8,128)(2,1)S(1)}, bf16[7,32,128]{2,1,0:T(8,128)(2,1)S(1)}, u32[]{:S(2)}, u32[]{:S(2)}) collective-permute-start(bf16[7,32,128]{2,1,0:T(8,128)(2,1)S(1)} %pad_maximum_fusion.refs_0_), channel_id=1, source_target_pairs={{0,5},{1,4},{2,7},{3,6},{4,1},{5,0},{6,3},{7,2},{8,13},{9,12},{10,... | collective-permute-start | bytes 172040 | tf_op jit(solution)/shard_map/ppermute | solution.py:186
  8.8 9.0 %collective-permute-start.3 = (bf16[7,32,128]{2,1,0:T(8,128)(2,1)S(1)}, bf16[7,32,128]{2,1,0:T(8,128)(2,1)S(1)}, u32[]{:S(2)}, u32[]{:S(2)}) collective-permute-start(bf16[7,32,128]{2,1,0:T(8,128)(2,1)S(1)} %pad_maximum_fusion.refs_0_), channel_id=1, source_target_pairs={{0,4},{1,5},{2,6},{3,7},{4,0},{5,1},{6,2},{7,3},{8,12},{9,13},{10,... | collective-permute-start | bytes 172040 | tf_op jit(solution)/shard_map/ppermute | solution.py:186
  10.8 7.0 %collective-permute-start.2 = (bf16[7,32,128]{2,1,0:T(8,128)(2,1)S(1)}, bf16[7,32,128]{2,1,0:T(8,128)(2,1)S(1)}, u32[]{:S(2)}, u32[]{:S(2)}) collective-permute-start(bf16[7,32,128]{2,1,0:T(8,128)(2,1)S(1)} %pad_maximum_fusion.refs_0_), channel_id=1, source_target_pairs={{0,3},{1,2},{2,1},{3,0},{4,7},{5,6},{6,5},{7,4},{8,11},{9,10},{10,... | collective-permute-start | bytes 172040 | tf_op jit(solution)/shard_map/ppermute | solution.py:186
  13.1 5.2 %collective-permute-start.1 = (bf16[7,32,128]{2,1,0:T(8,128)(2,1)S(1)}, bf16[7,32,128]{2,1,0:T(8,128)(2,1)S(1)}, u32[]{:S(2)}, u32[]{:S(2)}) collective-permute-start(bf16[7,32,128]{2,1,0:T(8,128)(2,1)S(1)} %pad_maximum_fusion.refs_0_), channel_id=1, source_target_pairs={{0,2},{1,3},{2,0},{3,1},{4,6},{5,7},{6,4},{7,5},{8,10},{9,11},{10,... | collective-permute-start | bytes 172040 | tf_op jit(solution)/shard_map/ppermute | solution.py:186
  13.9 4.4 %collective-permute-start = (bf16[7,32,128]{2,1,0:T(8,128)(2,1)S(1)}, bf16[7,32,128]{2,1,0:T(8,128)(2,1)S(1)}, u32[]{:S(2)}, u32[]{:S(2)}) collective-permute-start(bf16[7,32,128]{2,1,0:T(8,128)(2,1)S(1)} %pad_maximum_fusion.refs_0_), channel_id=1, source_target_pairs={{0,1},{1,0},{2,3},{3,2},{4,5},{5,4},{6,7},{7,6},{8,9},{9,8},{10,11... | collective-permute-start | bytes 172040 | tf_op jit(solution)/shard_map/ppermute | solution.py:186
  18.3 5.0 %collective-permute-start.8 = (bf16[2,8,32,128]{3,2,1,0:T(8,128)(2,1)S(1)}, bf16[2,8,32,128]{3,2,1,0:T(8,128)(2,1)S(1)}, u32[]{:S(2)}, u32[]{:S(2)}) collective-permute-start(bf16[2,8,32,128]{3,2,1,0:T(8,128)(2,1)S(1)} %pick.1.refs_1_), channel_id=1, source_target_pairs={{0,16},{8,24},{16,0},{24,8},{1,17},{9,25},{17,1},{25,9},{2,18},{10... | collective-permute-start | bytes 393224 | tf_op jit(solution)/shard_map/ppermute | solution.py:207
  19.9 5.5 %collective-permute-start.7 = (bf16[2,8,32,128]{3,2,1,0:T(8,128)(2,1)S(1)}, bf16[2,8,32,128]{3,2,1,0:T(8,128)(2,1)S(1)}, u32[]{:S(2)}, u32[]{:S(2)}) collective-permute-start(bf16[2,8,32,128]{3,2,1,0:T(8,128)(2,1)S(1)} %pick.1.refs_1_), channel_id=1, source_target_pairs={{0,8},{8,0},{16,24},{24,16},{1,9},{9,1},{17,25},{25,17},{2,10},{10... | collective-permute-start | bytes 393224 | tf_op jit(solution)/shard_map/ppermute | solution.py:207
  23.3 2.1 %collective-permute-start.9 = (bf16[2,8,32,128]{3,2,1,0:T(8,128)(2,1)S(1)}, bf16[2,8,32,128]{3,2,1,0:T(8,128)(2,1)S(1)}, u32[]{:S(2)}, u32[]{:S(2)}) collective-permute-start(bf16[2,8,32,128]{3,2,1,0:T(8,128)(2,1)S(1)} %collective-permute-done.8.refs_3_), channel_id=1, source_target_pairs={{0,8},{8,0},{16,24},{24,16},{1,9},{9,1},{17,25},{25,17},{2,10},{10... | collective-permute-start | bytes 393224 | tf_op jit(solution)/shard_map/ppermute | solution.py:207
  23.4 1.0 %copy-start.1 = (bf16[512,512]{1,0:T(8,128)(2,1)S(1)}, bf16[512,512]{1,0:T(8,128)(2,1)}, u32[]{:S(2)}) copy-start(bf16[512,512]{1,0:T(8,128)(2,1)} %refs_5_.1) | copy-start | bytes 1572868
  25.4 1.0 %copy-start.2 = (bf16[512,512]{1,0:T(8,128)(2,1)S(1)}, bf16[512,512]{1,0:T(8,128)(2,1)}, u32[]{:S(2)}) copy-start(bf16[512,512]{1,0:T(8,128)(2,1)} %refs_5_.1) | copy-start | bytes 1572868
where the time goes:
time: 33.6 us; the launch traced here: 33.3 us
  starting transfers between devices  14.2 us (42%)
  Pallas kernels  7.8 us (23%)
  waiting for transfers between devices  6.7 us (20%)
  local copies, waits for them, and re-layouts  2.4 us (7%)
  between operations  2.1 us (6%)
    ppermute x7, starting transfers between devices, step(): lax.ppermute(packed, 'col', [(c, c ^ k) for c in range(col_count)])  12.6 us
    pallas_call x1, Pallas kernels, step(): pl.pallas_call(functools.partial(main_kernel, peers, row_count, fold, dim...  6.84 us
    ppermute x3, waiting for transfers between devices, step(): lax.ppermute(sources[source], 'row', [(r, r ^ bit) for r in range(row_cou...  3.43 us
    ppermute x7, waiting for transfers between devices, step(): lax.ppermute(packed, 'col', [(c, c ^ k) for c in range(col_count)])  3.26 us
    unnamed x6, local copies, waits for them, and re-layouts  2.3 us
    ppermute x3, starting transfers between devices, step(): lax.ppermute(sources[source], 'row', [(r, r ^ bit) for r in range(row_cou...  1.61 us
    pallas_call x1, Pallas kernels, step(): left, factor_t = prep(*chunks, inverse_factor)  0.94 us
  transfers between devices with their start and end apart: 10, of which 5 were waited for; matrix products, arithmetic and copies ran while one was open for 0% of the time, Pallas kernels for 3%

commit v1 on v0

--- a/solution.py
+++ b/solution.py
@@ -69,7 +69,7 @@
 
 def prep_kernel(peers, fold, dim, *refs):
     chunks = refs[:peers]
-    factor, left, factor_t = refs[peers:]
+    factor, left, factor_copy, factor_t = refs[peers:]
     half = chunks[0].shape[1]
     width = fold * dim
     for k in range(peers):
@@ -77,6 +77,7 @@
         for part, norm in enumerate(half_norms(packed, fold, dim)):
             rows = with_norms(packed[:, part * dim : (part + 1) * dim], norm, None, 1.0, dim)
             left[k, :, part * half : (part + 1) * half, :] = rows.reshape(RW, half, LANES)
+    factor_copy[...] = factor[...]
     factor_t[...] = factor[...].T
 
 
@@ -84,7 +85,7 @@
     left = refs[0]
     held = refs[1 : 1 + sources]
     factor, factor_t, panel_out, update_out = refs[1 + sources : 5 + sources]
-    right_p, right_j, left_j, mat, kip, ent, obuf, sem = refs[5 + sources :]
+    right_p, right_j, left_j, mat, kip, ent, obuf, pbuf, sem, panel_sem = refs[5 + sources :]
     side = factor.shape[0]
     share = left.shape[2]
     half = share // fold
@@ -140,11 +141,12 @@
     steps = peers // group
     lcol = by_factor(kjp)
     kernels(0)
-    panel_out[...] = by_factor(kip[0, : RW * share]).reshape(RW, share, side)
+    pbuf[...] = by_factor(kip[0, : RW * share]).reshape(RW, share, side)
+    copies = [pltpu.make_async_copy(pbuf, panel_out, panel_sem)]
+    copies[0].start()
     mat[:cut] = dot(factor_t[:cut], lcol, NT).astype(jnp.bfloat16)
     mat[cut:] = dot(factor_t[cut:, cut:], lcol[:, cut:], NT).astype(jnp.bfloat16)
 
-    copies = []
     for step in range(steps):
         if step + 1 < steps:
             kernels(step + 1)
@@ -226,9 +228,10 @@
         out_shape=(
             jax.ShapeDtypeStruct((peers, RW, share, LANES), jnp.bfloat16),
             jax.ShapeDtypeStruct((side, side), jnp.bfloat16),
+            jax.ShapeDtypeStruct((side, side), jnp.bfloat16),
         ),
         in_specs=[vmem] * (peers + 1),
-        out_specs=(vmem, vmem),
+        out_specs=(vmem, vmem, vmem),
         compiler_params=pltpu.CompilerParams(vmem_limit_bytes=8 << 20),
         cost_estimate=pl.CostEstimate(
             flops=4 * peers * RW * half * LANES * LANES,
@@ -237,7 +240,7 @@
         ),
         name="prep",
     )
-    left, factor_t = prep(*chunks, inverse_factor)
+    left, factor, factor_t = prep(*chunks, inverse_factor)
     panel_part, update = pl.pallas_call(
         functools.partial(main_kernel, peers, row_count, fold, dim, group),
         out_shape=(
@@ -245,7 +248,7 @@
             jax.ShapeDtypeStruct((RW, side, side), jnp.bfloat16),
         ),
         in_specs=[smem] + [vmem] * (row_count + 3),
-        out_specs=(vmem, pl.BlockSpec(memory_space=pl.ANY)),
+        out_specs=(pl.BlockSpec(memory_space=pl.ANY), pl.BlockSpec(memory_space=pl.ANY)),
         scratch_shapes=[
             pltpu.VMEM((side, LANES), jnp.bfloat16),
             pltpu.VMEM((side, LANES), jnp.bfloat16),
@@ -254,11 +257,13 @@
             pltpu.VMEM((2, group * rows, side), jnp.bfloat16),
             pltpu.VMEM((2, group * rows, side), jnp.float32),
             pltpu.VMEM((steps, group, RW, share, side), jnp.bfloat16),
+            pltpu.VMEM((RW, share, side), jnp.bfloat16),
             pltpu.SemaphoreType.DMA((steps, group)),
+            pltpu.SemaphoreType.DMA,
         ],
         compiler_params=pltpu.CompilerParams(vmem_limit_bytes=40 << 20),
         name="tiles",
-    )(scalars, left, *sources, inverse_factor, factor_t)
+    )(scalars, left, *sources, factor, factor_t)
     return panel_part[:, None], update[:, None, :, None, :]
 
 

time: 33.6 us -> 31.7 us (0.943)
  local copies, waits for them, and re-layouts: 2.4 us -> 1.37 us
  Pallas kernels: 7.8 us -> 7.07 us
    unnamed x6 -> x4, local copies, waits for them, and re-layouts: 2.3 us -> 1.27 us
    pallas_call x1, Pallas kernels: 6.84 us -> 6.12 us  [step(): pl.pallas_call(functools.partial(main_kernel, peers, row_count, fold, dim...]
where the time goes in v1:
time: 31.7 us; the launch traced here: 31.5 us
  starting transfers between devices  14.2 us (45%)
  Pallas kernels  7.07 us (22%)
  waiting for transfers between devices  6.7 us (21%)
  between operations  2.09 us (7%)
  local copies, waits for them, and re-layouts  1.37 us (4%)
    ppermute x7, starting transfers between devices, step(): lax.ppermute(packed, 'col', [(c, c ^ k) for c in range(col_count)])  12.6 us
    pallas_call x1, Pallas kernels, step(): pl.pallas_call(functools.partial(main_kernel, peers, row_count, fold, dim...  6.12 us
    ppermute x3, waiting for transfers between devices, step(): lax.ppermute(sources[source], 'row', [(r, r ^ bit) for r in range(row_cou...  3.43 us
    ppermute x7, waiting for transfers between devices, step(): lax.ppermute(packed, 'col', [(c, c ^ k) for c in range(col_count)])  3.26 us
    ppermute x3, starting transfers between devices, step(): lax.ppermute(sources[source], 'row', [(r, r ^ bit) for r in range(row_cou...  1.61 us
    unnamed x4, local copies, waits for them, and re-layouts  1.27 us
    pallas_call x1, Pallas kernels, step(): left, factor, factor_t = prep(*chunks, inverse_factor)  0.94 us
  transfers between devices with their start and end apart: 10, of which 5 were waited for; matrix products, arithmetic and copies ran while one was open for 0% of the time, Pallas kernels for 3%

profile of v1, /device:TPU:0, one launch (start us, length us, event | category | flops | bytes accessed | tf_op | source)
XLA Modules:
  0.0 31.5 jit_solution(3541917248043954612)
XLA Ops:
  0.6 0.0 copy-start
  1.4 0.2 copy-done
  1.6 0.1 pad_maximum_fusion.refs_0_
  1.7 6.1 %collective-permute-start.6 = (bf16[7,32,128]{2,1,0:T(8,128)(2,1)S(1)}, bf16[7,32,128]{2,1,0:T(8,128)(2,1)S(1)}, u32[]{:S(2)}, u32[]{:S(2)}) collective-permute-start(bf16[7,32,128]{2,1,0:T(8,128)(2,1)S(1)} %pad_maximum_fusion.refs_0_), channel_id=1, source_target_pairs={{0,7},{1,6},{2,5},{3,4},{4,3},{5,2},{6,1},{7,0},{8,15},{9,14},{10,... | collective-permute-start | bytes 172040 | tf_op jit(solution)/shard_map/ppermute | solution.py:188
  7.8 0.2 collective-permute-start.5
  8.0 0.7 %collective-permute-start.4 = (bf16[7,32,128]{2,1,0:T(8,128)(2,1)S(1)}, bf16[7,32,128]{2,1,0:T(8,128)(2,1)S(1)}, u32[]{:S(2)}, u32[]{:S(2)}) collective-permute-start(bf16[7,32,128]{2,1,0:T(8,128)(2,1)S(1)} %pad_maximum_fusion.refs_0_), channel_id=1, source_target_pairs={{0,5},{1,4},{2,7},{3,6},{4,1},{5,0},{6,3},{7,2},{8,13},{9,12},{10,... | collective-permute-start | bytes 172040 | tf_op jit(solution)/shard_map/ppermute | solution.py:188
  8.8 2.0 %collective-permute-start.3 = (bf16[7,32,128]{2,1,0:T(8,128)(2,1)S(1)}, bf16[7,32,128]{2,1,0:T(8,128)(2,1)S(1)}, u32[]{:S(2)}, u32[]{:S(2)}) collective-permute-start(bf16[7,32,128]{2,1,0:T(8,128)(2,1)S(1)} %pad_maximum_fusion.refs_0_), channel_id=1, source_target_pairs={{0,4},{1,5},{2,6},{3,7},{4,0},{5,1},{6,2},{7,3},{8,12},{9,13},{10,... | collective-permute-start | bytes 172040 | tf_op jit(solution)/shard_map/ppermute | solution.py:188
  10.8 2.3 %collective-permute-start.2 = (bf16[7,32,128]{2,1,0:T(8,128)(2,1)S(1)}, bf16[7,32,128]{2,1,0:T(8,128)(2,1)S(1)}, u32[]{:S(2)}, u32[]{:S(2)}) collective-permute-start(bf16[7,32,128]{2,1,0:T(8,128)(2,1)S(1)} %pad_maximum_fusion.refs_0_), channel_id=1, source_target_pairs={{0,3},{1,2},{2,1},{3,0},{4,7},{5,6},{6,5},{7,4},{8,11},{9,10},{10,... | collective-permute-start | bytes 172040 | tf_op jit(solution)/shard_map/ppermute | solution.py:188
  13.1 0.0 collective-permute-done.6.refs_7_
  13.1 0.8 %collective-permute-start.1 = (bf16[7,32,128]{2,1,0:T(8,128)(2,1)S(1)}, bf16[7,32,128]{2,1,0:T(8,128)(2,1)S(1)}, u32[]{:S(2)}, u32[]{:S(2)}) collective-permute-start(bf16[7,32,128]{2,1,0:T(8,128)(2,1)S(1)} %pad_maximum_fusion.refs_0_), channel_id=1, source_target_pairs={{0,2},{1,3},{2,0},{3,1},{4,6},{5,7},{6,4},{7,5},{8,10},{9,11},{10,... | collective-permute-start | bytes 172040 | tf_op jit(solution)/shard_map/ppermute | solution.py:188
  13.9 0.0 collective-permute-done.5.refs_6_
  13.9 0.4 %collective-permute-start = (bf16[7,32,128]{2,1,0:T(8,128)(2,1)S(1)}, bf16[7,32,128]{2,1,0:T(8,128)(2,1)S(1)}, u32[]{:S(2)}, u32[]{:S(2)}) collective-permute-start(bf16[7,32,128]{2,1,0:T(8,128)(2,1)S(1)} %pad_maximum_fusion.refs_0_), channel_id=1, source_target_pairs={{0,1},{1,0},{2,3},{3,2},{4,5},{5,4},{6,7},{7,6},{8,9},{9,8},{10,11... | collective-permute-start | bytes 172040 | tf_op jit(solution)/shard_map/ppermute | solution.py:188
  15.0 1.3 %collective-permute-done.4.refs_5_ = bf16[7,32,128]{2,1,0:T(8,128)(2,1)S(1)} collective-permute-done((bf16[7,32,128]{2,1,0:T(8,128)(2,1)S(1)}, bf16[7,32,128]{2,1,0:T(8,128)(2,1)S(1)}, u32[]{:S(2)}, u32[]{:S(2)}) %collective-permute-start.4) | collective-permute-done | bytes 57376 | tf_op jit(solution)/shard_map/ppermute | solution.py:188
  16.3 1.5 %collective-permute-done.3.refs_4_ = bf16[7,32,128]{2,1,0:T(8,128)(2,1)S(1)} collective-permute-done((bf16[7,32,128]{2,1,0:T(8,128)(2,1)S(1)}, bf16[7,32,128]{2,1,0:T(8,128)(2,1)S(1)}, u32[]{:S(2)}, u32[]{:S(2)}) %collective-permute-start.3) | collective-permute-done | bytes 57376 | tf_op jit(solution)/shard_map/ppermute | solution.py:188
  17.7 0.1 collective-permute-done.2.refs_3_
  17.8 0.4 %collective-permute-done.1.refs_2_ = bf16[7,32,128]{2,1,0:T(8,128)(2,1)S(1)} collective-permute-done((bf16[7,32,128]{2,1,0:T(8,128)(2,1)S(1)}, bf16[7,32,128]{2,1,0:T(8,128)(2,1)S(1)}, u32[]{:S(2)}, u32[]{:S(2)}) %collective-permute-start.1) | collective-permute-done | bytes 57376 | tf_op jit(solution)/shard_map/ppermute | solution.py:188
  18.3 0.0 collective-permute-done.refs_1_
  18.3 1.6 %collective-permute-start.8 = (bf16[2,8,32,128]{3,2,1,0:T(8,128)(2,1)S(1)}, bf16[2,8,32,128]{3,2,1,0:T(8,128)(2,1)S(1)}, u32[]{:S(2)}, u32[]{:S(2)}) collective-permute-start(bf16[2,8,32,128]{3,2,1,0:T(8,128)(2,1)S(1)} %pick.1.refs_1_), channel_id=1, source_target_pairs={{0,16},{8,24},{16,0},{24,8},{1,17},{9,25},{17,1},{25,9},{2,18},{10... | collective-permute-start | bytes 393224 | tf_op jit(solution)/shard_map/ppermute | solution.py:209
  19.9 0.0 collective-permute-start.7
  19.9 3.4 %collective-permute-done.8.refs_3_ = bf16[2,8,32,128]{3,2,1,0:T(8,128)(2,1)S(1)} collective-permute-done((bf16[2,8,32,128]{3,2,1,0:T(8,128)(2,1)S(1)}, bf16[2,8,32,128]{3,2,1,0:T(8,128)(2,1)S(1)}, u32[]{:S(2)}, u32[]{:S(2)}) %collective-permute-start.8) | collective-permute-done | bytes 131104 | tf_op jit(solution)/shard_map/ppermute | solution.py:209
  23.3 0.0 collective-permute-start.9
  23.3 0.1 stack.27.scalars
  23.4 0.0 copy-start.1
  23.4 1.0 %copy-done.1 = bf16[512,512]{1,0:T(8,128)(2,1)S(1)} copy-done((bf16[512,512]{1,0:T(8,128)(2,1)S(1)}, bf16[512,512]{1,0:T(8,128)(2,1)}, u32[]{:S(2)}) %copy-start.1) | copy-done | bytes 524312
  24.5 0.9 %prep.1 = (bf16[8,6,64,128]{3,2,1,0:T(8,128)(2,1)S(1)}, bf16[512,512]{1,0:T(8,128)(2,1)S(1)}, bf16[512,512]{1,0:T(8,128)(2,1)S(1)}) custom-call(bf16[7,32,128]{2,1,0:T(8,128)(2,1)S(1)} %pad_maximum_fusion.refs_0_, bf16[7,32,128]{2,1,0:T(8,128)(2,1)S(1)} %collective-permute-done.refs_1_, bf16[7,32,128]{2,1,0:T(8,128)(2,1)S(1)} %collective-permute-done.1.refs_2_, ...), custom_call_target="tpu_custom_call" | custom-call | flops 100663296 | bytes 1572864 | tf_op jit(solution)/shard_map/prep/pallas_call | solution.py:243
  25.4 0.0 collective-permute-done.7.refs_2_
  25.4 0.0 collective-permute-done.9.refs_4_
  25.4 6.1 %tiles.1 = (bf16[6,64,512]{2,1,0:T(8,128)(2,1)}, bf16[6,512,512]{2,1,0:T(8,128)(2,1)}) custom-call(s32[5]{0:T(128)S(1)} %stack.27.scalars, bf16[8,6,64,128]{3,2,1,0:T(8,128)(2,1)S(1)} %get-tuple-element.7.refs_0_, bf16[2,8,32,128]{3,2,1,0:T(8,128)(2,1)S(1)} %pick.1.refs_1_, bf16[2,8,32,128]{3,2,1,0:T(8,128)(2,1)S(1)} %collective-permute-done.7.refs_2_, ...), custom_call_target="tpu_custom_call" | custom-call | tf_op jit(solution)/shard_map/tiles/pallas_call | solution.py:244
  (3 shorter events, 0.0 us)
Async XLA Ops:
  0.6 0.9 %copy-start = (bf16[12,1,64,64]{3,2,1,0:T(8,128)(2,1)S(1)}, bf16[12,1,64,64]{3,2,1,0:T(8,128)(2,1)}, u32[]{:S(2)}) copy-start(bf16[12,1,64,64]{3,2,1,0:T(8,128)(2,1)} %param.4) | copy-start | bytes 294916
  1.7 11.4 %collective-permute-start.6 = (bf16[7,32,128]{2,1,0:T(8,128)(2,1)S(1)}, bf16[7,32,128]{2,1,0:T(8,128)(2,1)S(1)}, u32[]{:S(2)}, u32[]{:S(2)}) collective-permute-start(bf16[7,32,128]{2,1,0:T(8,128)(2,1)S(1)} %pad_maximum_fusion.refs_0_), channel_id=1, source_target_pairs={{0,7},{1,6},{2,5},{3,4},{4,3},{5,2},{6,1},{7,0},{8,15},{9,14},{10,... | collective-permute-start | bytes 172040 | tf_op jit(solution)/shard_map/ppermute | solution.py:188
  7.8 6.1 %collective-permute-start.5 = (bf16[7,32,128]{2,1,0:T(8,128)(2,1)S(1)}, bf16[7,32,128]{2,1,0:T(8,128)(2,1)S(1)}, u32[]{:S(2)}, u32[]{:S(2)}) collective-permute-start(bf16[7,32,128]{2,1,0:T(8,128)(2,1)S(1)} %pad_maximum_fusion.refs_0_), channel_id=1, source_target_pairs={{0,6},{1,7},{2,4},{3,5},{4,2},{5,3},{6,0},{7,1},{8,14},{9,15},{10,... | collective-permute-start | bytes 172040 | tf_op jit(solution)/shard_map/ppermute | solution.py:188
  8.0 8.2 %collective-permute-start.4 = (bf16[7,32,128]{2,1,0:T(8,128)(2,1)S(1)}, bf16[7,32,128]{2,1,0:T(8,128)(2,1)S(1)}, u32[]{:S(2)}, u32[]{:S(2)}) collective-permute-start(bf16[7,32,128]{2,1,0:T(8,128)(2,1)S(1)} %pad_maximum_fusion.refs_0_), channel_id=1, source_target_pairs={{0,5},{1,4},{2,7},{3,6},{4,1},{5,0},{6,3},{7,2},{8,13},{9,12},{10,... | collective-permute-start | bytes 172040 | tf_op jit(solution)/shard_map/ppermute | solution.py:188
  8.8 9.0 %collective-permute-start.3 = (bf16[7,32,128]{2,1,0:T(8,128)(2,1)S(1)}, bf16[7,32,128]{2,1,0:T(8,128)(2,1)S(1)}, u32[]{:S(2)}, u32[]{:S(2)}) collective-permute-start(bf16[7,32,128]{2,1,0:T(8,128)(2,1)S(1)} %pad_maximum_fusion.refs_0_), channel_id=1, source_target_pairs={{0,4},{1,5},{2,6},{3,7},{4,0},{5,1},{6,2},{7,3},{8,12},{9,13},{10,... | collective-permute-start | bytes 172040 | tf_op jit(solution)/shard_map/ppermute | solution.py:188
  10.8 7.0 %collective-permute-start.2 = (bf16[7,32,128]{2,1,0:T(8,128)(2,1)S(1)}, bf16[7,32,128]{2,1,0:T(8,128)(2,1)S(1)}, u32[]{:S(2)}, u32[]{:S(2)}) collective-permute-start(bf16[7,32,128]{2,1,0:T(8,128)(2,1)S(1)} %pad_maximum_fusion.refs_0_), channel_id=1, source_target_pairs={{0,3},{1,2},{2,1},{3,0},{4,7},{5,6},{6,5},{7,4},{8,11},{9,10},{10,... | collective-permute-start | bytes 172040 | tf_op jit(solution)/shard_map/ppermute | solution.py:188
  13.1 5.2 %collective-permute-start.1 = (bf16[7,32,128]{2,1,0:T(8,128)(2,1)S(1)}, bf16[7,32,128]{2,1,0:T(8,128)(2,1)S(1)}, u32[]{:S(2)}, u32[]{:S(2)}) collective-permute-start(bf16[7,32,128]{2,1,0:T(8,128)(2,1)S(1)} %pad_maximum_fusion.refs_0_), channel_id=1, source_target_pairs={{0,2},{1,3},{2,0},{3,1},{4,6},{5,7},{6,4},{7,5},{8,10},{9,11},{10,... | collective-permute-start | bytes 172040 | tf_op jit(solution)/shard_map/ppermute | solution.py:188
  13.9 4.4 %collective-permute-start = (bf16[7,32,128]{2,1,0:T(8,128)(2,1)S(1)}, bf16[7,32,128]{2,1,0:T(8,128)(2,1)S(1)}, u32[]{:S(2)}, u32[]{:S(2)}) collective-permute-start(bf16[7,32,128]{2,1,0:T(8,128)(2,1)S(1)} %pad_maximum_fusion.refs_0_), channel_id=1, source_target_pairs={{0,1},{1,0},{2,3},{3,2},{4,5},{5,4},{6,7},{7,6},{8,9},{9,8},{10,11... | collective-permute-start | bytes 172040 | tf_op jit(solution)/shard_map/ppermute | solution.py:188
  18.3 5.0 %collective-permute-start.8 = (bf16[2,8,32,128]{3,2,1,0:T(8,128)(2,1)S(1)}, bf16[2,8,32,128]{3,2,1,0:T(8,128)(2,1)S(1)}, u32[]{:S(2)}, u32[]{:S(2)}) collective-permute-start(bf16[2,8,32,128]{3,2,1,0:T(8,128)(2,1)S(1)} %pick.1.refs_1_), channel_id=1, source_target_pairs={{0,16},{8,24},{16,0},{24,8},{1,17},{9,25},{17,1},{25,9},{2,18},{10... | collective-permute-start | bytes 393224 | tf_op jit(solution)/shard_map/ppermute | solution.py:209
  19.9 5.5 %collective-permute-start.7 = (bf16[2,8,32,128]{3,2,1,0:T(8,128)(2,1)S(1)}, bf16[2,8,32,128]{3,2,1,0:T(8,128)(2,1)S(1)}, u32[]{:S(2)}, u32[]{:S(2)}) collective-permute-start(bf16[2,8,32,128]{3,2,1,0:T(8,128)(2,1)S(1)} %pick.1.refs_1_), channel_id=1, source_target_pairs={{0,8},{8,0},{16,24},{24,16},{1,9},{9,1},{17,25},{25,17},{2,10},{10... | collective-permute-start | bytes 393224 | tf_op jit(solution)/shard_map/ppermute | solution.py:209
  23.3 2.1 %collective-permute-start.9 = (bf16[2,8,32,128]{3,2,1,0:T(8,128)(2,1)S(1)}, bf16[2,8,32,128]{3,2,1,0:T(8,128)(2,1)S(1)}, u32[]{:S(2)}, u32[]{:S(2)}) collective-permute-start(bf16[2,8,32,128]{3,2,1,0:T(8,128)(2,1)S(1)} %collective-permute-done.8.refs_3_), channel_id=1, source_target_pairs={{0,8},{8,0},{16,24},{24,16},{1,9},{9,1},{17,25},{25,17},{2,10},{10... | collective-permute-start | bytes 393224 | tf_op jit(solution)/shard_map/ppermute | solution.py:209
  23.4 1.0 %copy-start.1 = (bf16[512,512]{1,0:T(8,128)(2,1)S(1)}, bf16[512,512]{1,0:T(8,128)(2,1)}, u32[]{:S(2)}) copy-start(bf16[512,512]{1,0:T(8,128)(2,1)} %refs_8_.1) | copy-start | bytes 1572868

commit v2 on v1

v2 whole, which is shorter than its diff:
```python
import functools

import jax
import jax.numpy as jnp
from jax import lax
from jax.experimental import pallas as pl
from jax.experimental.pallas import tpu as pltpu
from jax.sharding import PartitionSpec as P


RW = 6
JITTER = 1.0
LANES = 128


NT = (((1,), (1,)), ((), ()))
NN = (((1,), (0,)), ((), ()))


def dot(left, right, dims):
    return lax.dot_general(left, right, dims, preferred_element_type=jnp.float32)


PIECES = 3


def pieces_of(values):
    pieces = []
    for _ in range(PIECES):
        piece = values.astype(jnp.bfloat16)
        pieces.append(piece)
        values = values - piece.astype(jnp.float32)
    return pieces


def split_squares(points):
    vals = points.astype(jnp.float32)
    squares = vals * vals
    high = squares.astype(jnp.bfloat16)
    low = (squares - high.astype(jnp.float32)).astype(jnp.bfloat16)
    return jnp.concatenate([high, low], axis=1)


def half_norms(packed, fold, dim):
    width = fold * dim
    part_of_row = (lax.broadcasted_iota(jnp.int32, (2 * width, fold * LANES), 0) % width) // dim
    part_of_lane = lax.broadcasted_iota(jnp.int32, (2 * width, fold * LANES), 1) // LANES
    mask = jnp.where(part_of_row == part_of_lane, 0.5, 0.0).astype(jnp.bfloat16)
    norms = dot(split_squares(packed), mask, NN)
    return [norms[:, part * LANES : (part + 1) * LANES] for part in range(fold)]


def with_norms(points, norm, dim):
    rows = points.shape[0]
    lane = lax.broadcasted_iota(jnp.int32, (rows, LANES - dim), 1)
    tail = jnp.zeros((rows, LANES - dim), jnp.float32)
    for n, piece in enumerate(pieces_of(norm[:, : LANES - dim])):
        tail = jnp.where(lane == n, piece.astype(jnp.float32), tail)
    return jnp.concatenate([points, tail.astype(jnp.bfloat16)], axis=1)


def pick_kernel(count, scalars, *refs):
    mine, held, (windows, cands) = refs[:2], refs[2 : 2 + count], refs[2 + count :]
    core = scalars[0]
    for i in range(count):
        rows = [held[i][line] for line in range(2)]
        if i == 0:
            rows = [jnp.where(core > 0, rows[line], mine[line][...]) for line in range(2)]
        windows[i] = rows[1][1:]
        for which in range(2):
            other = scalars[1 + which] > 0
            if which == 0:
                cands[i, which] = jnp.where(other, rows[1][0], rows[0][0])
            else:
                picks = []
                for line in range(2):
                    pick = rows[line][1]
                    for slot in range(1, RW):
                        pick = jnp.where(scalars[3 + line] == slot, rows[line][1 + slot], pick)
                    picks.append(pick)
                cands[i, which] = jnp.where(other, picks[1], picks[0])


def prep_kernel(count, fold, dim, evens, scalars, *refs):
    mine, held, windows, factor, left, factor_copy, factor_t = (
        refs[0], refs[1 : 1 + count], refs[1 + count], *refs[2 + count :]
    )
    half = mine.shape[1]
    width = fold * dim
    core = scalars[0]
    for i in range(2 * count):
        if i == 0:
            packed = jnp.where(core > 0, held[0][0], mine[...])[1:]
        elif i < count:
            packed = held[i][0, 1:]
        else:
            packed = windows[i - count]
        at = evens[i % count] ^ core if i < count else evens[i % count] ^ 1 ^ core
        packed = packed.reshape(RW * half, width)
        for part, norm in enumerate(half_norms(packed, fold, dim)):
            rows = with_norms(packed[:, part * dim : (part + 1) * dim], norm, dim)
            left[at, :, part * half : (part + 1) * half, :] = rows.reshape(RW, half, LANES)
    factor_copy[...] = factor[...]
    factor_t[...] = factor[...].T


def main_kernel(peers, sources, fold, dim, group, evens, scalars, *refs):
    left = refs[0]
    held, flipped = refs[1 : 1 + sources], refs[1 + sources : 1 + 2 * sources]
    refs = refs[1 + 2 * sources :]
    factor, factor_t, panel_out, update_out = refs[:4]
    right_p, right_j, mat, kip, ent, obuf, pbuf, sem, panel_sem = refs[4:]
    side = factor.shape[0]
    share = left.shape[2]
    half = share // fold
    cut = side // 2
    col_here = scalars[0]
    scale = 1.0 / dim

    tail = jnp.where(
        lax.broadcasted_iota(jnp.int32, (half, LANES - dim), 1) < PIECES, -scale, 0.0
    ).astype(jnp.bfloat16)
    for which, right in ((0, right_p), (1, right_j)):
        source = scalars[1 + which]
        for k in range(peers):
            i, lists = k % (peers // 2), (held if k < peers // 2 else flipped)
            distance = evens[i] ^ scalars[5] ^ (0 if k < peers // 2 else 1)
            block = lists[0][i, which]
            for other in range(1, sources):
                block = jnp.where(source == other, lists[other][i, which], block)
            block = (block.astype(jnp.float32) * scale).astype(jnp.bfloat16)
            for part in range(fold):
                start = pl.multiple_of((col_here ^ distance) * share + part * half, half)
                points = block[:, part * dim : (part + 1) * dim]
                right[pl.ds(start, half), :] = jnp.concatenate([points, tail], axis=1)

    lane = lax.broadcasted_iota(jnp.int32, (8, 2 * LANES), 1) % LANES
    weight = jnp.where(lane < dim, dim / 2.0, 0.0).astype(jnp.bfloat16)
    squares_j = split_squares(right_j[...])
    norm_p = dot(weight, split_squares(right_p[...]), NT)[:1]
    norm_j = dot(weight, squares_j, NT)[:1]
    lane = lax.broadcasted_iota(jnp.int32, (2 * LANES, LANES), 0) % LANES
    weight = jnp.where(lane < dim, dim / 2.0, 0.0).astype(jnp.bfloat16)
    rows_j = dot(squares_j, weight, NN)[:, :1]

    lane = lax.broadcasted_iota(jnp.int32, (side, LANES), 1)
    bare_j = jnp.where(lane < dim, right_j[...].astype(jnp.float32) * dim, 0.0).astype(jnp.bfloat16)
    kjp = jnp.exp(dot(bare_j, right_p[...], NT) - rows_j - norm_p).astype(jnp.bfloat16)

    def by_factor(values):
        return jnp.concatenate(
            [
                dot(values[:, :cut], factor[:cut, :cut], NT),
                dot(values, factor[cut:, :], NT),
            ],
            axis=1,
        ).astype(jnp.bfloat16)

    def kernels(step):
        members = left[pl.ds(step * group, group)].reshape(group * RW * share, LANES)
        slot = step % 2
        kip[slot] = jnp.exp(dot(members, right_p[...], NT) - norm_p).astype(jnp.bfloat16)
        ent[slot] = jnp.exp(dot(members, right_j[...], NT) - norm_j)
        for m in range(group):
            row0 = (col_here ^ (step * group + m)) * share
            lane0 = pl.multiple_of((row0 // LANES) * LANES, LANES)
            at = pl.ds(pl.multiple_of((m * RW + scalars[3]) * share, share), share)
            rows = lax.broadcasted_iota(jnp.int32, (share, LANES), 0) + row0
            cols = lax.broadcasted_iota(jnp.int32, (share, LANES), 1) + lane0
            hit = (rows == cols) & (scalars[4] > 0)
            ent[slot, at, pl.ds(lane0, LANES)] += jnp.where(hit, JITTER, 0.0)

    def out_copy(step, m):
        row0 = pl.multiple_of((col_here ^ (step * group + m)) * share, share)
        return pltpu.make_async_copy(
            obuf.at[step, m], update_out.at[:, pl.ds(row0, share), :], sem.at[step, m]
        )

    def finish(step):
        slot = step % 2
        result = (ent[slot] - dot(kip[slot], mat[...], NN)).astype(jnp.bfloat16)
        obuf[step] = result.reshape(group, RW, share, side)
        for m in range(group):
            out_copy(step, m).start()

    steps = peers // group
    lcol = by_factor(kjp)
    kernels(0)
    mat[:cut] = dot(factor_t[:cut], lcol, NT).astype(jnp.bfloat16)
    mat[cut:] = dot(factor_t[cut:, cut:], lcol[:, cut:], NT).astype(jnp.bfloat16)
    pbuf[...] = by_factor(kip[0, : RW * share]).reshape(RW, share, side)
    panel_copy = pltpu.make_async_copy(pbuf, panel_out, panel_sem)
    panel_copy.start()

    for step in range(steps - 1):
        kernels(step + 1)
        finish(step)

    finish(steps - 1)
    panel_copy.wait()
    for step in range(steps):
        for m in range(group):
            out_copy(step, m).wait()


def step(points, inverse_factor, panel_index, column_map):
    row_count = lax.axis_size("row")
    col_count = lax.axis_size("col")
    row_here = lax.axis_index("row")
    col_here = lax.axis_index("col")
    side = inverse_factor.shape[0]
    share, dim = points.shape[2], points.shape[3]
    fold = max(1, LANES // dim)
    half = share // fold
    peers = col_count
    group = min(1, peers)
    rows = RW * share

    pivot_tile = panel_index[0]
    start_slot = (pivot_tile + row_count - row_here) // row_count
    local_points = lax.dynamic_slice_in_dim(points[:, 0], start_slot - 1, RW + 1, 0)
    packed = jnp.concatenate(
        [local_points[:, part * half : (part + 1) * half] for part in range(fold)], axis=-1
    )
    evens = [d for d in range(col_count) if d.bit_count() % 2 == 0]
    count = len(evens)
    core = row_here & 1
    flip = [(r, r ^ 1) for r in range(row_count)]
    both = jnp.stack([packed, lax.ppermute(packed, "row", flip)])
    held = [None] * count
    for i in range(count - 1, -1, -1):
        pairs = [
            (r * col_count + c, r * col_count + (c ^ evens[i] ^ (r & 1)))
            for r in range(row_count)
            for c in range(col_count)
            if evens[i] ^ (r & 1)
        ]
        held[i] = lax.ppermute(both, ("row", "col"), pairs)

    column_tile = pivot_tile + 1 + column_map[0]
    panel_owner = pivot_tile % row_count
    column_owner = column_tile % row_count

    def slot_of(row):
        first = (pivot_tile + row_count - row) // row_count
        return jnp.clip(column_tile // row_count - first, 0, RW - 1)

    position = slot_of(row_here)
    vmem = pl.BlockSpec(memory_space=pltpu.VMEM)
    smem = pl.BlockSpec(memory_space=pltpu.SMEM)
    scalars = jnp.stack(
        [
            core,
            (panel_owner ^ row_here) & 1,
            (column_owner ^ row_here) & 1,
            position,
            slot_of(row_here ^ 1),
        ]
    ).astype(jnp.int32)
    windows, cands = pl.pallas_call(
        functools.partial(pick_kernel, count),
        out_shape=(
            jax.ShapeDtypeStruct((count, RW, half, fold * dim), jnp.bfloat16),
            jax.ShapeDtypeStruct((count, 2, half, fold * dim), jnp.bfloat16),
        ),
        in_specs=[smem] + [vmem] * (2 + count),
        out_specs=(vmem, vmem),
        compiler_params=pltpu.CompilerParams(vmem_limit_bytes=4 << 20),
        name="pick",
    )(scalars, both[0], both[1], *held)

    sources = {0: cands}
    bit = row_count >> 1
    while bit > 1:
        for source in sorted(sources, reverse=True):
            sources[source ^ bit] = lax.ppermute(
                sources[source], "row", [(r, r ^ bit) for r in range(row_count)]
            )
        bit >>= 1
    sources = [sources[source] for source in range(0, row_count, 2)]
    windows = lax.ppermute(windows, "row", flip)
    flipped = [lax.ppermute(source, "row", flip) for source in sources]

    diag_slot = jnp.where(column_owner == row_here, position, 0)
    tile_scalars = jnp.stack(
        [
            col_here,
            (panel_owner ^ row_here) >> 1,
            (column_owner ^ row_here) >> 1,
            diag_slot,
            (column_owner == row_here).astype(jnp.int32),
            core,
        ]
    ).astype(jnp.int32)
    steps = peers // group
    prep = pl.pallas_call(
        functools.partial(prep_kernel, count, fold, dim, evens),
        out_shape=(
            jax.ShapeDtypeStruct((peers, RW, share, LANES), jnp.bfloat16),
            jax.ShapeDtypeStruct((side, side), jnp.bfloat16),
            jax.ShapeDtypeStruct((side, side), jnp.bfloat16),
        ),
        in_specs=[smem] + [vmem] * (count + 3),
        out_specs=(vmem, vmem, vmem),
        compiler_params=pltpu.CompilerParams(vmem_limit_bytes=8 << 20),
        cost_estimate=pl.CostEstimate(
            flops=4 * peers * RW * half * LANES * LANES,
            bytes_accessed=4 * peers * rows * LANES,
            transcendentals=0,
        ),
        name="prep",
    )
    left, factor, factor_t = prep(scalars, packed, *held, windows, inverse_factor)
    panel_part, update = pl.pallas_call(
        functools.partial(main_kernel, peers, row_count // 2, fold, dim, group, evens),
        out_shape=(
            jax.ShapeDtypeStruct((RW, share, side), jnp.bfloat16),
            jax.ShapeDtypeStruct((RW, side, side), jnp.bfloat16),
        ),
        in_specs=[smem] + [vmem] * (row_count + 3),
        out_specs=(pl.BlockSpec(memory_space=pl.ANY), pl.BlockSpec(memory_space=pl.ANY)),
        scratch_shapes=[
            pltpu.VMEM((side, LANES), jnp.bfloat16),
            pltpu.VMEM((side, LANES), jnp.bfloat16),
            pltpu.VMEM((side, side), jnp.bfloat16),
            pltpu.VMEM((2, group * rows, side), jnp.bfloat16),
            pltpu.VMEM((2, group * rows, side), jnp.float32),
            pltpu.VMEM((steps, group, RW, share, side), jnp.bfloat16),
            pltpu.VMEM((RW, share, side), jnp.bfloat16),
            pltpu.SemaphoreType.DMA((steps, group)),
            pltpu.SemaphoreType.DMA,
        ],
        compiler_params=pltpu.CompilerParams(vmem_limit_bytes=40 << 20),
        name="tiles",
    )(tile_scalars, left, *sources, *flipped, factor, factor_t)
    return panel_part[:, None], update[:, None, :, None, :]


def solution(mesh):
    in_specs = (P(None, "row", "col", None), P(), P(), P("col"))
    out_specs = (P(None, "row", "col", None), P(None, "row", None, "col", None))
    return jax.shard_map(step, mesh=mesh, in_specs=in_specs, out_specs=out_specs, check_vma=False)
```

time: 31.7 us -> 33 us (1.041)
  waiting for transfers between devices: 6.7 us -> 11.6 us
  starting transfers between devices: 14.2 us -> 9.54 us
  Pallas kernels: 7.07 us -> 7.97 us
    ppermute x7 -> x8, waiting for transfers between devices: 3.26 us -> 8.77 us  [the longest x4 7.87 us: step(): held[i] = lax.ppermute(both, ('row', 'col'), pairs)]
    ppermute x7 -> x8, starting transfers between devices: 12.6 us -> 8 us  [the longest x4 7.2 us: step(): held[i] = lax.ppermute(both, ('row', 'col'), pairs)]
    pallas_call x3, Pallas kernels: 7.07 us -> 7.97 us  [the longest x1 5.9 us: step(): pl.pallas_call(functools.partial(main_kernel, peers, row_count // 2, fold...]
    ppermute x3 -> x1, waiting for transfers between devices: 3.43 us -> 2.79 us  [step(): lax.ppermute(sources[source], 'row', [(r, r ^ bit) for r in range(row_cou...]
    ppermute x3 -> x1, starting transfers between devices: 1.61 us -> 1.54 us  [step(): lax.ppermute(sources[source], 'row', [(r, r ^ bit) for r in range(row_cou...]
  transfers between devices with their start and end apart: 10 -> 9, of which waited for: 5 -> 4; matrix products, arithmetic and copies ran while one was open for 0% -> 1% of each run, Pallas kernels for 3% -> 4%
where the time goes in v2:
time: 33 us; the launch traced here: 32.8 us
  waiting for transfers between devices  11.6 us (35%)
  starting transfers between devices  9.54 us (29%)
  Pallas kernels  7.97 us (24%)
  between operations  2.15 us (7%)
  local copies, waits for them, and re-layouts  1.46 us (4%)
    ppermute x4, waiting for transfers between devices, step(): held[i] = lax.ppermute(both, ('row', 'col'), pairs)  7.87 us
    ppermute x4, starting transfers between devices, step(): held[i] = lax.ppermute(both, ('row', 'col'), pairs)  7.2 us
    pallas_call x1, Pallas kernels, step(): pl.pallas_call(functools.partial(main_kernel, peers, row_count // 2, fold...  5.9 us
    ppermute x1, waiting for transfers between devices, step(): lax.ppermute(sources[source], 'row', [(r, r ^ bit) for r in range(row_cou...  2.79 us
    ppermute x1, starting transfers between devices, step(): lax.ppermute(sources[source], 'row', [(r, r ^ bit) for r in range(row_cou...  1.54 us
    pallas_call x1, Pallas kernels, step(): prep(scalars, packed, *held, windows, inverse_factor)  1.45 us
    unnamed x4, local copies, waits for them, and re-layouts  1.27 us
    ppermute x1, waiting for transfers between devices, step(): both = jnp.stack([packed, lax.ppermute(packed, 'row', flip)])  0.89 us
  transfers between devices with their start and end apart: 9, of which 4 were waited for; matrix products, arithmetic and copies ran while one was open for 1% of the time, Pallas kernels for 4%

profile of v2, /device:TPU:0, one launch (start us, length us, event | category | flops | bytes accessed | tf_op | source)
XLA Modules:
  0.0 32.8 jit_solution(9708964602567580773)
XLA Ops:
  0.6 0.0 copy-start
  1.4 0.2 copy-done
  1.6 0.1 pad_maximum_fusion.1.refs_0_
  1.7 0.6 %collective-permute-start = (bf16[7,32,128]{2,1,0:T(8,128)(2,1)S(1)}, bf16[7,32,128]{2,1,0:T(8,128)(2,1)S(1)}, u32[]{:S(2)}, u32[]{:S(2)}) collective-permute-start(bf16[7,32,128]{2,1,0:T(8,128)(2,1)S(1)} %pad_maximum_fusion.1.refs_0_), channel_id=1, source_target_pairs={{0,8},{8,0},{16,24},{24,16},{1,9},{9,1},{17,25},{25,17},{2,10},{10... | collective-permute-start | bytes 172040 | tf_op jit(solution)/shard_map/ppermute | solution.py:229
  2.3 0.9 %collective-permute-done.refs_1_ = bf16[7,32,128]{2,1,0:T(8,128)(2,1)S(1)} collective-permute-done((bf16[7,32,128]{2,1,0:T(8,128)(2,1)S(1)}, bf16[7,32,128]{2,1,0:T(8,128)(2,1)S(1)}, u32[]{:S(2)}, u32[]{:S(2)}) %collective-permute-start) | collective-permute-done | bytes 57376 | tf_op jit(solution)/shard_map/ppermute | solution.py:229
  3.2 5.0 %collective-permute-start.4 = (bf16[2,7,32,128]{3,2,1,0:T(8,128)(2,1)S(1)}, bf16[2,7,32,128]{3,2,1,0:T(8,128)(2,1)S(1)}, u32[]{:S(2)}, u32[]{:S(2)}) collective-permute-start(bf16[2,7,32,128]{3,2,1,0:T(8,128)(2,1)S(1)} %pad_maximum_fusion), channel_id=1, source_target_pairs={{0,6},{1,7},{2,4},{3,5},{4,2},{5,3},{6,0},{7,1},{8,15},{9,14},{10,... | collective-permute-start | bytes 344072 | tf_op jit(solution)/shard_map/ppermute | solution.py:238
  8.2 0.4 %collective-permute-start.3 = (bf16[2,7,32,128]{3,2,1,0:T(8,128)(2,1)S(1)}, bf16[2,7,32,128]{3,2,1,0:T(8,128)(2,1)S(1)}, u32[]{:S(2)}, u32[]{:S(2)}) collective-permute-start(bf16[2,7,32,128]{3,2,1,0:T(8,128)(2,1)S(1)} %pad_maximum_fusion), channel_id=1, source_target_pairs={{0,5},{1,4},{2,7},{3,6},{4,1},{5,0},{6,3},{7,2},{8,12},{9,13},{10,... | collective-permute-start | bytes 344072 | tf_op jit(solution)/shard_map/ppermute | solution.py:238
  8.6 1.1 %collective-permute-start.2 = (bf16[2,7,32,128]{3,2,1,0:T(8,128)(2,1)S(1)}, bf16[2,7,32,128]{3,2,1,0:T(8,128)(2,1)S(1)}, u32[]{:S(2)}, u32[]{:S(2)}) collective-permute-start(bf16[2,7,32,128]{3,2,1,0:T(8,128)(2,1)S(1)} %pad_maximum_fusion), channel_id=1, source_target_pairs={{0,3},{1,2},{2,1},{3,0},{4,7},{5,6},{6,5},{7,4},{8,10},{9,11},{10,... | collective-permute-start | bytes 344072 | tf_op jit(solution)/shard_map/ppermute | solution.py:238
  9.7 0.7 %collective-permute-start.1 = (bf16[2,7,32,128]{3,2,1,0:T(8,128)(2,1)S(1)}, bf16[2,7,32,128]{3,2,1,0:T(8,128)(2,1)S(1)}, u32[]{:S(2)}, u32[]{:S(2)}) collective-permute-start(bf16[2,7,32,128]{3,2,1,0:T(8,128)(2,1)S(1)} %pad_maximum_fusion), channel_id=1, source_target_pairs={{8,9},{9,8},{10,11},{11,10},{12,13},{13,12},{14,15},{15,14},{24,25... | collective-permute-start | bytes 344072 | tf_op jit(solution)/shard_map/ppermute | solution.py:238
  11.1 0.1 stack.61.scalars
  11.2 0.7 %collective-permute-done.4.refs_5_.refs_4_ = bf16[2,7,32,128]{3,2,1,0:T(8,128)(2,1)S(1)} collective-permute-done((bf16[2,7,32,128]{3,2,1,0:T(8,128)(2,1)S(1)}, bf16[2,7,32,128]{3,2,1,0:T(8,128)(2,1)S(1)}, u32[]{:S(2)}, u32[]{:S(2)}) %collective-permute-start.4) | collective-permute-done | bytes 114720 | tf_op jit(solution)/shard_map/ppermute | solution.py:238
  11.9 7.1 %collective-permute-done.3.refs_4_.refs_3_ = bf16[2,7,32,128]{3,2,1,0:T(8,128)(2,1)S(1)} collective-permute-done((bf16[2,7,32,128]{3,2,1,0:T(8,128)(2,1)S(1)}, bf16[2,7,32,128]{3,2,1,0:T(8,128)(2,1)S(1)}, u32[]{:S(2)}, u32[]{:S(2)}) %collective-permute-start.3) | collective-permute-done | bytes 114720 | tf_op jit(solution)/shard_map/ppermute | solution.py:238
  19.1 0.0 collective-permute-done.2.refs_3_.refs_2_
  19.1 0.0 collective-permute-done.1.refs_2_.refs_1_
  19.1 0.6 %pick.1 = (bf16[4,6,32,128]{3,2,1,0:T(8,128)(2,1)S(1)}, bf16[4,2,32,128]{3,2,1,0:T(8,128)(2,1)S(1)}) custom-call(s32[5]{0:T(128)S(1)} %stack.61.scalars, bf16[7,32,128]{2,1,0:T(8,128)(2,1)S(1)} %pad_maximum_fusion.1.refs_0_, bf16[7,32,128]{2,1,0:T(8,128)(2,1)S(1)} %collective-permute-done.refs_1_, ...), custom_call_target="tpu_custom_call" | custom-call | tf_op jit(solution)/shard_map/pick/pallas_call | solution.py:260
  19.7 0.1 collective-permute-start.5
  19.8 1.5 %collective-permute-start.6 = (bf16[4,2,32,128]{3,2,1,0:T(8,128)(2,1)S(1)}, bf16[4,2,32,128]{3,2,1,0:T(8,128)(2,1)S(1)}, u32[]{:S(2)}, u32[]{:S(2)}) collective-permute-start(bf16[4,2,32,128]{3,2,1,0:T(8,128)(2,1)S(1)} %get-tuple-element.11.refs_1_), channel_id=1, source_target_pairs={{0,16},{8,24},{16,0},{24,8},{1,17},{9,25},{17,1},{25,9},{2,18},{10... | collective-permute-start | bytes 196616 | tf_op jit(solution)/shard_map/ppermute | solution.py:276
  21.3 0.2 collective-permute-start.7
  21.5 2.8 %collective-permute-done.6.refs_2_ = bf16[4,2,32,128]{3,2,1,0:T(8,128)(2,1)S(1)} collective-permute-done((bf16[4,2,32,128]{3,2,1,0:T(8,128)(2,1)S(1)}, bf16[4,2,32,128]{3,2,1,0:T(8,128)(2,1)S(1)}, u32[]{:S(2)}, u32[]{:S(2)}) %collective-permute-start.6) | collective-permute-done | bytes 65568 | tf_op jit(solution)/shard_map/ppermute | solution.py:276
  24.3 0.0 collective-permute-start.8
  24.3 0.1 stack.56.scalars
  24.4 0.0 collective-permute-done.5.refs_5_
  24.4 0.0 copy-start.1
  24.4 1.0 %copy-done.1 = bf16[512,512]{1,0:T(8,128)(2,1)S(1)} copy-done((bf16[512,512]{1,0:T(8,128)(2,1)S(1)}, bf16[512,512]{1,0:T(8,128)(2,1)}, u32[]{:S(2)}) %copy-start.1) | copy-done | bytes 524312
  25.4 1.4 %prep.1 = (bf16[8,6,64,128]{3,2,1,0:T(8,128)(2,1)S(1)}, bf16[512,512]{1,0:T(8,128)(2,1)S(1)}, bf16[512,512]{1,0:T(8,128)(2,1)S(1)}) custom-call(s32[5]{0:T(128)S(1)} %stack.61.scalars, bf16[7,32,128]{2,1,0:T(8,128)(2,1)S(1)} %pad_maximum_fusion.1.refs_0_, bf16[2,7,32,128]{3,2,1,0:T(8,128)(2,1)S(1)} %collective-permute-done.1.refs_2_.refs_1_, ...), custom_call_target="tpu_custom_call" | custom-call | flops 100663296 | bytes 1572864 | tf_op jit(solution)/shard_map/prep/pallas_call | solution.py:313
  26.9 0.0 collective-permute-done.7.refs_3_
  26.9 0.0 collective-permute-done.8.refs_4_
  26.9 5.9 %tiles.1 = (bf16[6,64,512]{2,1,0:T(8,128)(2,1)}, bf16[6,512,512]{2,1,0:T(8,128)(2,1)}) custom-call(s32[6]{0:T(128)S(1)} %stack.56.scalars, bf16[8,6,64,128]{3,2,1,0:T(8,128)(2,1)S(1)} %get-tuple-element.10.refs_0_, bf16[4,2,32,128]{3,2,1,0:T(8,128)(2,1)S(1)} %get-tuple-element.11.refs_1_, bf16[4,2,32,128]{3,2,1,0:T(8,128)(2,1)S(1)} %collective-permute-done.6.refs_2_, ...), custom_call_target="tpu_custom_call" | custom-call | tf_op jit(solution)/shard_map/tiles/pallas_call | solution.py:314
  (3 shorter events, 0.0 us)
Async XLA Ops:
  0.6 0.9 %copy-start = (bf16[12,1,64,64]{3,2,1,0:T(8,128)(2,1)S(1)}, bf16[12,1,64,64]{3,2,1,0:T(8,128)(2,1)}, u32[]{:S(2)}) copy-start(bf16[12,1,64,64]{3,2,1,0:T(8,128)(2,1)} %param.4) | copy-start | bytes 294916
  1.7 1.4 %collective-permute-start = (bf16[7,32,128]{2,1,0:T(8,128)(2,1)S(1)}, bf16[7,32,128]{2,1,0:T(8,128)(2,1)S(1)}, u32[]{:S(2)}, u32[]{:S(2)}) collective-permute-start(bf16[7,32,128]{2,1,0:T(8,128)(2,1)S(1)} %pad_maximum_fusion.1.refs_0_), channel_id=1, source_target_pairs={{0,8},{8,0},{16,24},{24,16},{1,9},{9,1},{17,25},{25,17},{2,10},{10... | collective-permute-start | bytes 172040 | tf_op jit(solution)/shard_map/ppermute | solution.py:229
  3.2 8.8 %collective-permute-start.4 = (bf16[2,7,32,128]{3,2,1,0:T(8,128)(2,1)S(1)}, bf16[2,7,32,128]{3,2,1,0:T(8,128)(2,1)S(1)}, u32[]{:S(2)}, u32[]{:S(2)}) collective-permute-start(bf16[2,7,32,128]{3,2,1,0:T(8,128)(2,1)S(1)} %pad_maximum_fusion), channel_id=1, source_target_pairs={{0,6},{1,7},{2,4},{3,5},{4,2},{5,3},{6,0},{7,1},{8,15},{9,14},{10,... | collective-permute-start | bytes 344072 | tf_op jit(solution)/shard_map/ppermute | solution.py:238
  8.2 10.9 %collective-permute-start.3 = (bf16[2,7,32,128]{3,2,1,0:T(8,128)(2,1)S(1)}, bf16[2,7,32,128]{3,2,1,0:T(8,128)(2,1)S(1)}, u32[]{:S(2)}, u32[]{:S(2)}) collective-permute-start(bf16[2,7,32,128]{3,2,1,0:T(8,128)(2,1)S(1)} %pad_maximum_fusion), channel_id=1, source_target_pairs={{0,5},{1,4},{2,7},{3,6},{4,1},{5,0},{6,3},{7,2},{8,12},{9,13},{10,... | collective-permute-start | bytes 344072 | tf_op jit(solution)/shard_map/ppermute | solution.py:238
  8.6 10.5 %collective-permute-start.2 = (bf16[2,7,32,128]{3,2,1,0:T(8,128)(2,1)S(1)}, bf16[2,7,32,128]{3,2,1,0:T(8,128)(2,1)S(1)}, u32[]{:S(2)}, u32[]{:S(2)}) collective-permute-start(bf16[2,7,32,128]{3,2,1,0:T(8,128)(2,1)S(1)} %pad_maximum_fusion), channel_id=1, source_target_pairs={{0,3},{1,2},{2,1},{3,0},{4,7},{5,6},{6,5},{7,4},{8,10},{9,11},{10,... | collective-permute-start | bytes 344072 | tf_op jit(solution)/shard_map/ppermute | solution.py:238
  9.7 9.4 %collective-permute-start.1 = (bf16[2,7,32,128]{3,2,1,0:T(8,128)(2,1)S(1)}, bf16[2,7,32,128]{3,2,1,0:T(8,128)(2,1)S(1)}, u32[]{:S(2)}, u32[]{:S(2)}) collective-permute-start(bf16[2,7,32,128]{3,2,1,0:T(8,128)(2,1)S(1)} %pad_maximum_fusion), channel_id=1, source_target_pairs={{8,9},{9,8},{10,11},{11,10},{12,13},{13,12},{14,15},{15,14},{24,25... | collective-permute-start | bytes 344072 | tf_op jit(solution)/shard_map/ppermute | solution.py:238
  19.7 4.7 %collective-permute-start.5 = (bf16[4,6,32,128]{3,2,1,0:T(8,128)(2,1)S(1)}, bf16[4,6,32,128]{3,2,1,0:T(8,128)(2,1)S(1)}, u32[]{:S(2)}, u32[]{:S(2)}) collective-permute-start(bf16[4,6,32,128]{3,2,1,0:T(8,128)(2,1)S(1)} %get-tuple-element.9), channel_id=1, source_target_pairs={{0,8},{8,0},{16,24},{24,16},{1,9},{9,1},{17,25},{25,17},{2,10},{10... | collective-permute-start | bytes 589832 | tf_op jit(solution)/shard_map/ppermute | solution.py:281
  19.8 4.5 %collective-permute-start.6 = (bf16[4,2,32,128]{3,2,1,0:T(8,128)(2,1)S(1)}, bf16[4,2,32,128]{3,2,1,0:T(8,128)(2,1)S(1)}, u32[]{:S(2)}, u32[]{:S(2)}) collective-permute-start(bf16[4,2,32,128]{3,2,1,0:T(8,128)(2,1)S(1)} %get-tuple-element.11.refs_1_), channel_id=1, source_target_pairs={{0,16},{8,24},{16,0},{24,8},{1,17},{9,25},{17,1},{25,9},{2,18},{10... | collective-permute-start | bytes 196616 | tf_op jit(solution)/shard_map/ppermute | solution.py:276
  21.3 5.5 %collective-permute-start.7 = (bf16[4,2,32,128]{3,2,1,0:T(8,128)(2,1)S(1)}, bf16[4,2,32,128]{3,2,1,0:T(8,128)(2,1)S(1)}, u32[]{:S(2)}, u32[]{:S(2)}) collective-permute-start(bf16[4,2,32,128]{3,2,1,0:T(8,128)(2,1)S(1)} %get-tuple-element.11.refs_1_), channel_id=1, source_target_pairs={{0,8},{8,0},{16,24},{24,16},{1,9},{9,1},{17,25},{25,17},{2,10},{10... | collective-permute-start | bytes 196616 | tf_op jit(solution)/shard_map/ppermute | solution.py:282
  24.3 2.6 %collective-permute-start.8 = (bf16[4,2,32,128]{3,2,1,0:T(8,128)(2,1)S(1)}, bf16[4,2,32,128]{3,2,1,0:T(8,128)(2,1)S(1)}, u32[]{:S(2)}, u32[]{:S(2)}) collective-permute-start(bf16[4,2,32,128]{3,2,1,0:T(8,128)(2,1)S(1)} %collective-permute-done.6.refs_2_), channel_id=1, source_target_pairs={{0,8},{8,0},{16,24},{24,16},{1,9},{9,1},{17,25},{25,17},{2,10},{10... | collective-permute-start | bytes 196616 | tf_op jit(solution)/shard_map/ppermute | solution.py:282
  24.4 1.0 %copy-start.1 = (bf16[512,512]{1,0:T(8,128)(2,1)S(1)}, bf16[512,512]{1,0:T(8,128)(2,1)}, u32[]{:S(2)}) copy-start(bf16[512,512]{1,0:T(8,128)(2,1)} %refs_6_.1) | copy-start | bytes 1572868

commit v3 on v2

v3 whole, which is shorter than its diff:
```python
import functools

import jax
import jax.numpy as jnp
from jax import lax
from jax.experimental import pallas as pl
from jax.experimental.pallas import tpu as pltpu
from jax.sharding import PartitionSpec as P


RW = 6
JITTER = 1.0
LANES = 128


NT = (((1,), (1,)), ((), ()))
NN = (((1,), (0,)), ((), ()))


def dot(left, right, dims):
    return lax.dot_general(left, right, dims, preferred_element_type=jnp.float32)


PIECES = 3


def pieces_of(values):
    pieces = []
    for _ in range(PIECES):
        piece = values.astype(jnp.bfloat16)
        pieces.append(piece)
        values = values - piece.astype(jnp.float32)
    return pieces


def split_squares(points):
    vals = points.astype(jnp.float32)
    squares = vals * vals
    high = squares.astype(jnp.bfloat16)
    low = (squares - high.astype(jnp.float32)).astype(jnp.bfloat16)
    return jnp.concatenate([high, low], axis=1)


def half_norms(packed, fold, dim):
    width = fold * dim
    part_of_row = (lax.broadcasted_iota(jnp.int32, (2 * width, fold * LANES), 0) % width) // dim
    part_of_lane = lax.broadcasted_iota(jnp.int32, (2 * width, fold * LANES), 1) // LANES
    mask = jnp.where(part_of_row == part_of_lane, 0.5, 0.0).astype(jnp.bfloat16)
    norms = dot(split_squares(packed), mask, NN)
    return [norms[:, part * LANES : (part + 1) * LANES] for part in range(fold)]


def with_norms(points, norm, dim):
    rows = points.shape[0]
    lane = lax.broadcasted_iota(jnp.int32, (rows, LANES - dim), 1)
    tail = jnp.zeros((rows, LANES - dim), jnp.float32)
    for n, piece in enumerate(pieces_of(norm[:, : LANES - dim])):
        tail = jnp.where(lane == n, piece.astype(jnp.float32), tail)
    return jnp.concatenate([points, tail.astype(jnp.bfloat16)], axis=1)


FIELD = 8


def packed_scalars(*values):
    code = jnp.int32(0)
    for value in reversed(values):
        code = (code << FIELD) + value.astype(jnp.int32)
    return code[None]


def unpacked(scalars, number):
    return [(scalars[0] >> (FIELD * n)) & ((1 << FIELD) - 1) for n in range(number)]


def pick_kernel(count, scalars, own, opposite, *refs):
    held, (windows, cands) = refs[:count], refs[count:]
    at, own_at = unpacked(scalars, 2)
    for i in range(count):
        cands[i, 0] = held[i][0]
        cands[i, 1] = held[i][at]
        windows[i] = held[i][1 + RW :]
    for i, block in ((count, own), (count + 1, opposite)):
        cands[i, 0] = block[0]
        cands[i, 1] = block[own_at]


def turn_kernel(factor, factor_copy, factor_t):
    factor_copy[...] = factor[...]
    factor_t[...] = factor[...].T


def prep_kernel(count, fold, dim, distances, scalars, own, opposite, *refs):
    held, (windows, left) = refs[:count], refs[count:]
    half = own.shape[1]
    width = fold * dim
    across = 2 * count + 1
    turned = scalars[0] * across
    blocks = [(own[1:], 0), (opposite[1:], across)]
    blocks += [(held[i][1 : 1 + RW], distances[i] ^ turned) for i in range(count)]
    blocks += [(windows[i], distances[i] ^ across ^ turned) for i in range(count)]
    for packed, at in blocks:
        packed = packed.reshape(RW * half, width)
        for part, norm in enumerate(half_norms(packed, fold, dim)):
            rows = with_norms(packed[:, part * dim : (part + 1) * dim], norm, dim)
            left[at, :, part * half : (part + 1) * half, :] = rows.reshape(RW, half, LANES)


def main_kernel(peers, sources, fold, dim, distances, places, aways, *refs):
    left = refs[0]
    held, flipped = refs[1 : 1 + sources], refs[1 + sources : 1 + 2 * sources]
    refs = refs[1 + 2 * sources :]
    factor, factor_t, panel_out, update_out = refs[:4]
    right_p, right_j, mat, kip, ent, obuf, pbuf, sem, panel_sem = refs[4:]
    side = factor.shape[0]
    share = left.shape[2]
    half = share // fold
    cut = side // 2
    col_here, diag_slot, flags = unpacked(places, 3)
    away = unpacked(aways, 2)
    core, holds = flags & 1, flags >> 1
    scale = 1.0 / dim

    tail = jnp.where(
        lax.broadcasted_iota(jnp.int32, (half, LANES - dim), 1) < PIECES, -scale, 0.0
    ).astype(jnp.bfloat16)

    def from_row(lists, i, which):
        block = lists[0][i, which]
        for other in range(1, sources):
            block = jnp.where(away[which] >> 1 == other, lists[other][i, which], block)
        return block

    count = len(distances)
    across = peers - 1
    turned = core * across
    for which, right in ((0, right_p), (1, right_j)):
        blocks = []
        for i, distance in enumerate(distances):
            blocks.append((from_row(held, i, which), distance ^ turned))
            blocks.append((from_row(flipped, i, which), distance ^ across ^ turned))
        for i, distance in ((count, 0), (count + 1, across)):
            near, far = from_row(held, i, which), from_row(flipped, i, which)
            blocks.append((jnp.where(away[which] & 1 > 0, far, near), distance))
        for block, distance in blocks:
            block = (block.astype(jnp.float32) * scale).astype(jnp.bfloat16)
            for part in range(fold):
                start = pl.multiple_of((col_here ^ distance) * share + part * half, half)
                points = block[:, part * dim : (part + 1) * dim]
                right[pl.ds(start, half), :] = jnp.concatenate([points, tail], axis=1)

    lane = lax.broadcasted_iota(jnp.int32, (8, 2 * LANES), 1) % LANES
    weight = jnp.where(lane < dim, dim / 2.0, 0.0).astype(jnp.bfloat16)
    squares_j = split_squares(right_j[...])
    norm_p = dot(weight, split_squares(right_p[...]), NT)[:1]
    norm_j = dot(weight, squares_j, NT)[:1]
    lane = lax.broadcasted_iota(jnp.int32, (2 * LANES, LANES), 0) % LANES
    weight = jnp.where(lane < dim, dim / 2.0, 0.0).astype(jnp.bfloat16)
    rows_j = dot(squares_j, weight, NN)[:, :1]

    lane = lax.broadcasted_iota(jnp.int32, (side, LANES), 1)
    bare_j = jnp.where(lane < dim, right_j[...].astype(jnp.float32) * dim, 0.0).astype(jnp.bfloat16)
    kjp = jnp.exp(dot(bare_j, right_p[...], NT) - rows_j - norm_p).astype(jnp.bfloat16)

    def by_factor(values):
        return jnp.concatenate(
            [
                dot(values[:, :cut], factor[:cut, :cut], NT),
                dot(values, factor[cut:, :], NT),
            ],
            axis=1,
        ).astype(jnp.bfloat16)

    def kernels(step):
        members = left[step].reshape(RW * share, LANES)
        slot = step % 2
        kip[slot] = jnp.exp(dot(members, right_p[...], NT) - norm_p).astype(jnp.bfloat16)
        ent[slot] = jnp.exp(dot(members, right_j[...], NT) - norm_j)
        row0 = (col_here ^ step) * share
        lane0 = pl.multiple_of((row0 // LANES) * LANES, LANES)
        at = pl.ds(pl.multiple_of(diag_slot * share, share), share)
        rows = lax.broadcasted_iota(jnp.int32, (share, LANES), 0) + row0
        cols = lax.broadcasted_iota(jnp.int32, (share, LANES), 1) + lane0
        hit = (rows == cols) & (holds > 0)
        ent[slot, at, pl.ds(lane0, LANES)] += jnp.where(hit, JITTER, 0.0)

    def out_copies(step):
        row0 = pl.multiple_of((col_here ^ step) * share, share)
        return [
            pltpu.make_async_copy(
                obuf.at[step], update_out.at[:, pl.ds(row0, share), :], sem.at[step, 0]
            )
        ]

    def finish(step):
        slot = step % 2
        result = (ent[slot] - dot(kip[slot], mat[...], NN)).astype(jnp.bfloat16)
        obuf[step] = result.reshape(RW, share, side)
        for copy in out_copies(step):
            copy.start()

    steps = peers
    lcol = by_factor(kjp)
    kernels(0)
    mat[:cut] = dot(factor_t[:cut], lcol, NT).astype(jnp.bfloat16)
    mat[cut:] = dot(factor_t[cut:, cut:], lcol[:, cut:], NT).astype(jnp.bfloat16)
    pbuf[...] = by_factor(kip[0]).reshape(RW, share, side)
    panel_copy = pltpu.make_async_copy(pbuf, panel_out, panel_sem)
    panel_copy.start()

    for step in range(steps - 1):
        kernels(step + 1)
        finish(step)

    finish(steps - 1)
    panel_copy.wait()
    for step in range(steps):
        for copy in out_copies(step):
            copy.wait()


def step(points, inverse_factor, panel_index, column_map):
    row_count = lax.axis_size("row")
    col_count = lax.axis_size("col")
    row_here = lax.axis_index("row")
    col_here = lax.axis_index("col")
    side = inverse_factor.shape[0]
    share, dim = points.shape[2], points.shape[3]
    fold = max(1, LANES // dim)
    half = share // fold
    peers = col_count
    rows = RW * share

    pivot_tile = panel_index[0]
    column_tile = pivot_tile + 1 + column_map[0]
    panel_away = (pivot_tile % row_count) ^ row_here
    column_away = (column_tile % row_count) ^ row_here

    def start_of(row):
        return (pivot_tile + row_count - row) // row_count

    local_points = lax.dynamic_slice_in_dim(points[:, 0], start_of(row_here) - 1, RW + 1, 0)
    packed = jnp.concatenate(
        [local_points[:, part * half : (part + 1) * half] for part in range(fold)], axis=-1
    )
    across = col_count - 1
    distances = [d for d in range(1, across) if d.bit_count() % 2 == 0]
    count = len(distances)
    core = row_here & 1
    flip = [(r, r ^ 1) for r in range(row_count)]
    other = lax.ppermute(packed, "row", flip)
    opposite = lax.ppermute(packed, "col", [(c, c ^ across) for c in range(col_count)])
    panel_slot = jnp.where(panel_away & 1 > 0, other[:1], packed[:1])
    mine = jnp.concatenate([panel_slot, packed[1:], other[1:]])
    held = [None] * count
    for i in range(count):
        pairs = [
            (r * col_count + c, r * col_count + (c ^ distances[i] ^ (across * (r & 1))))
            for r in range(row_count)
            for c in range(col_count)
        ]
        held[i] = lax.ppermute(mine, ("row", "col"), pairs)

    def slot_of(row):
        return jnp.clip(column_tile // row_count - start_of(row), 0, RW - 1)

    vmem = pl.BlockSpec(memory_space=pltpu.VMEM)
    smem = pl.BlockSpec(memory_space=pltpu.SMEM)
    line = column_away & 1
    slots = packed_scalars(1 + line * RW + slot_of(row_here ^ line), 1 + slot_of(row_here))
    windows, cands = pl.pallas_call(
        functools.partial(pick_kernel, count),
        out_shape=(
            jax.ShapeDtypeStruct((count, RW, half, fold * dim), jnp.bfloat16),
            jax.ShapeDtypeStruct((count + 2, 2, half, fold * dim), jnp.bfloat16),
        ),
        in_specs=[smem] + [vmem] * (2 + count),
        out_specs=(vmem, vmem),
        compiler_params=pltpu.CompilerParams(vmem_limit_bytes=4 << 20),
        name="pick",
    )(slots, packed, opposite, *held)

    sources = {0: cands}
    bit = row_count >> 1
    while bit > 1:
        for source in sorted(sources, reverse=True):
            sources[source ^ bit] = lax.ppermute(
                sources[source], "row", [(r, r ^ bit) for r in range(row_count)]
            )
        bit >>= 1
    sources = [sources[source] for source in range(0, row_count, 2)]
    windows = lax.ppermute(windows, "row", flip)
    flipped = [lax.ppermute(source, "row", flip) for source in sources]

    turn = pl.pallas_call(
        turn_kernel,
        out_shape=(
            jax.ShapeDtypeStruct((side, side), jnp.bfloat16),
            jax.ShapeDtypeStruct((side, side), jnp.bfloat16),
        ),
        in_specs=[vmem],
        out_specs=(vmem, vmem),
        compiler_params=pltpu.CompilerParams(vmem_limit_bytes=4 << 20),
        name="turn",
    )
    factor, factor_t = turn(inverse_factor)

    prep = pl.pallas_call(
        functools.partial(prep_kernel, count, fold, dim, distances),
        out_shape=jax.ShapeDtypeStruct((peers, RW, share, LANES), jnp.bfloat16),
        in_specs=[smem] + [vmem] * (3 + count),
        out_specs=vmem,
        compiler_params=pltpu.CompilerParams(vmem_limit_bytes=8 << 20),
        cost_estimate=pl.CostEstimate(
            flops=4 * peers * RW * half * LANES * LANES,
            bytes_accessed=4 * peers * rows * LANES,
            transcendentals=0,
        ),
        name="prep",
    )
    left = prep(core[None].astype(jnp.int32), packed, opposite, *held, windows)

    holds = column_away == 0
    places = packed_scalars(col_here, jnp.where(holds, slot_of(row_here), 0), core + 2 * holds)
    aways = packed_scalars(panel_away, column_away)
    panel_part, update = pl.pallas_call(
        functools.partial(main_kernel, peers, row_count // 2, fold, dim, distances),
        out_shape=(
            jax.ShapeDtypeStruct((RW, share, side), jnp.bfloat16),
            jax.ShapeDtypeStruct((RW, side, side), jnp.bfloat16),
        ),
        in_specs=[smem, smem] + [vmem] * (row_count + 3),
        out_specs=(pl.BlockSpec(memory_space=pl.ANY), pl.BlockSpec(memory_space=pl.ANY)),
        scratch_shapes=[
            pltpu.VMEM((side, LANES), jnp.bfloat16),
            pltpu.VMEM((side, LANES), jnp.bfloat16),
            pltpu.VMEM((side, side), jnp.bfloat16),
            pltpu.VMEM((2, rows, side), jnp.bfloat16),
            pltpu.VMEM((2, rows, side), jnp.float32),
            pltpu.VMEM((peers, RW, share, side), jnp.bfloat16),
            pltpu.VMEM((RW, share, side), jnp.bfloat16),
            pltpu.SemaphoreType.DMA((peers, RW)),
            pltpu.SemaphoreType.DMA,
        ],
        compiler_params=pltpu.CompilerParams(vmem_limit_bytes=40 << 20),
        name="tiles",
    )(places, aways, left, *sources, *flipped, factor, factor_t)
    return panel_part[:, None], update[:, None, :, None, :]


def solution(mesh):
    in_specs = (P(None, "row", "col", None), P(), P(), P("col"))
    out_specs = (P(None, "row", "col", None), P(None, "row", None, "col", None))
    return jax.shard_map(step, mesh=mesh, in_specs=in_specs, out_specs=out_specs, check_vma=False)
```

time: 33 us -> 31.3 us (0.948)
  waiting for transfers between devices: 11.6 us -> 6.82 us
  starting transfers between devices: 9.54 us -> 13.9 us
  Pallas kernels: 7.97 us -> 6.71 us
    ppermute x5, waiting for transfers between devices: 8.76 us -> 4.38 us  [the longest x1 2.78 us: step(): lax.ppermute(packed, 'col', [(c, c ^ across) for c in range(col_count)])]
    ppermute x5, starting transfers between devices: 7.76 us -> 11.8 us  [the longest x3 6.54 us: step(): held[i] = lax.ppermute(mine, ('row', 'col'), pairs)]
    pallas_call x1, Pallas kernels: 0.63 us -> 0.02 us  [step(): pl.pallas_call(functools.partial(pick_kernel, count), out_shape=(jax.Shap...]
    pallas_call x1 -> x2, Pallas kernels: 1.45 us -> 0.98 us  [the longest x1 0.8 us: step(): left = prep(core[None].astype(jnp.int32), packed, opposite, *held, windows)]
    ppermute x2, starting transfers between devices: 0.15 us -> 0.51 us  [step(): flipped = [lax.ppermute(source, 'row', flip) for source in sources]]
    ppermute x1, waiting for transfers between devices: 2.79 us -> 2.44 us  [step(): lax.ppermute(sources[source], 'row', [(r, r ^ bit) for r in range(row_cou...]
  transfers between devices with their start and end apart: 9 -> 9, of which waited for: 4 -> 4; matrix products, arithmetic and copies ran while one was open for 1% -> 0% of each run, Pallas kernels for 4% -> 3%
where the time goes in v3:
time: 31.3 us; the launch traced here: 31.1 us
  starting transfers between devices  13.9 us (44%)
  waiting for transfers between devices  6.82 us (22%)
  Pallas kernels  6.71 us (21%)
  between operations  2.16 us (7%)
  local copies, waits for them, and re-layouts  1.29 us (4%)
    ppermute x3, starting transfers between devices, step(): held[i] = lax.ppermute(mine, ('row', 'col'), pairs)  6.54 us
    pallas_call x1, Pallas kernels, step(): pl.pallas_call(functools.partial(main_kernel, peers, row_count // 2, fold...  5.71 us
    ppermute x1, starting transfers between devices, step(): lax.ppermute(packed, 'col', [(c, c ^ across) for c in range(col_count)])  4.7 us
    ppermute x1, waiting for transfers between devices, step(): lax.ppermute(packed, 'col', [(c, c ^ across) for c in range(col_count)])  2.78 us
    ppermute x1, waiting for transfers between devices, step(): lax.ppermute(sources[source], 'row', [(r, r ^ bit) for r in range(row_cou...  2.44 us
    ppermute x1, starting transfers between devices, step(): lax.ppermute(sources[source], 'row', [(r, r ^ bit) for r in range(row_cou...  1.56 us
    unnamed x4, local copies, waits for them, and re-layouts  1.26 us
    pallas_call x1, Pallas kernels, step(): left = prep(core[None].astype(jnp.int32), packed, opposite, *held, windows)  0.8 us
  transfers between devices with their start and end apart: 9, of which 4 were waited for; matrix products, arithmetic and copies ran while one was open for 0% of the time, Pallas kernels for 3%

profile of v3, /device:TPU:0, one launch (start us, length us, event | category | flops | bytes accessed | tf_op | source)
XLA Modules:
  0.0 31.1 jit_solution(18400187841594504879)
XLA Ops:
  0.6 0.0 copy-start
  1.4 0.2 copy-done
  1.6 0.1 pad_maximum_fusion.1.own
  1.7 0.6 %collective-permute-start.1 = (bf16[7,32,128]{2,1,0:T(8,128)(2,1)S(1)}, bf16[7,32,128]{2,1,0:T(8,128)(2,1)S(1)}, u32[]{:S(2)}, u32[]{:S(2)}) collective-permute-start(bf16[7,32,128]{2,1,0:T(8,128)(2,1)S(1)} %pad_maximum_fusion.1.own), channel_id=1, source_target_pairs={{0,8},{8,0},{16,24},{24,16},{1,9},{9,1},{17,25},{25,17},{2,10},{10... | collective-permute-start | bytes 172040 | tf_op jit(solution)/shard_map/ppermute | solution.py:251
  2.3 0.1 slice_maximum_fusion
  2.4 0.8 %collective-permute-done.1 = bf16[7,32,128]{2,1,0:T(8,128)(2,1)S(1)} collective-permute-done((bf16[7,32,128]{2,1,0:T(8,128)(2,1)S(1)}, bf16[7,32,128]{2,1,0:T(8,128)(2,1)S(1)}, u32[]{:S(2)}, u32[]{:S(2)}) %collective-permute-start.1) | collective-permute-done | bytes 57376 | tf_op jit(solution)/shard_map/ppermute | solution.py:251
  3.2 0.1 fusion.1
  3.3 5.0 %collective-permute-start.4 = (bf16[13,32,128]{2,1,0:T(8,128)(2,1)S(1)}, bf16[13,32,128]{2,1,0:T(8,128)(2,1)S(1)}, u32[]{:S(2)}, u32[]{:S(2)}) collective-permute-start(bf16[13,32,128]{2,1,0:T(8,128)(2,1)S(1)} %pad_maximum_fusion), channel_id=1, source_target_pairs={{0,6},{1,7},{2,4},{3,5},{4,2},{5,3},{6,0},{7,1},{8,9},{9,8},{10,11... | collective-permute-start | bytes 319496 | tf_op jit(solution)/shard_map/ppermute | solution.py:262
  8.3 0.4 %collective-permute-start.3 = (bf16[13,32,128]{2,1,0:T(8,128)(2,1)S(1)}, bf16[13,32,128]{2,1,0:T(8,128)(2,1)S(1)}, u32[]{:S(2)}, u32[]{:S(2)}) collective-permute-start(bf16[13,32,128]{2,1,0:T(8,128)(2,1)S(1)} %pad_maximum_fusion), channel_id=1, source_target_pairs={{0,5},{1,4},{2,7},{3,6},{4,1},{5,0},{6,3},{7,2},{8,10},{9,11},{10,... | collective-permute-start | bytes 319496 | tf_op jit(solution)/shard_map/ppermute | solution.py:262
  8.7 1.1 %collective-permute-start.2 = (bf16[13,32,128]{2,1,0:T(8,128)(2,1)S(1)}, bf16[13,32,128]{2,1,0:T(8,128)(2,1)S(1)}, u32[]{:S(2)}, u32[]{:S(2)}) collective-permute-start(bf16[13,32,128]{2,1,0:T(8,128)(2,1)S(1)} %pad_maximum_fusion), channel_id=1, source_target_pairs={{0,3},{1,2},{2,1},{3,0},{4,7},{5,6},{6,5},{7,4},{8,12},{9,13},{10,... | collective-permute-start | bytes 319496 | tf_op jit(solution)/shard_map/ppermute | solution.py:262
  9.8 4.7 %collective-permute-start = (bf16[7,32,128]{2,1,0:T(8,128)(2,1)S(1)}, bf16[7,32,128]{2,1,0:T(8,128)(2,1)S(1)}, u32[]{:S(2)}, u32[]{:S(2)}) collective-permute-start(bf16[7,32,128]{2,1,0:T(8,128)(2,1)S(1)} %pad_maximum_fusion.1.own), channel_id=1, source_target_pairs={{0,7},{1,6},{2,5},{3,4},{4,3},{5,2},{6,1},{7,0},{8,15},{9,14},{10,... | collective-permute-start | bytes 172040 | tf_op jit(solution)/shard_map/ppermute | solution.py:252
  15.2 2.8 %collective-permute-done.opposite = bf16[7,32,128]{2,1,0:T(8,128)(2,1)S(1)} collective-permute-done((bf16[7,32,128]{2,1,0:T(8,128)(2,1)S(1)}, bf16[7,32,128]{2,1,0:T(8,128)(2,1)S(1)}, u32[]{:S(2)}, u32[]{:S(2)}) %collective-permute-start) | collective-permute-done | bytes 57376 | tf_op jit(solution)/shard_map/ppermute | solution.py:252
  18.0 0.0 collective-permute-done.4.refs_2_
  18.0 0.8 %collective-permute-done.3.refs_1_ = bf16[13,32,128]{2,1,0:T(8,128)(2,1)S(1)} collective-permute-done((bf16[13,32,128]{2,1,0:T(8,128)(2,1)S(1)}, bf16[13,32,128]{2,1,0:T(8,128)(2,1)S(1)}, u32[]{:S(2)}, u32[]{:S(2)}) %collective-permute-start.3) | collective-permute-done | bytes 106528 | tf_op jit(solution)/shard_map/ppermute | solution.py:262
  18.8 0.0 collective-permute-done.2.refs_0_
  18.8 1.6 %collective-permute-start.6 = (bf16[5,2,32,128]{3,2,1,0:T(8,128)(2,1)S(1)}, bf16[5,2,32,128]{3,2,1,0:T(8,128)(2,1)S(1)}, u32[]{:S(2)}, u32[]{:S(2)}) collective-permute-start(bf16[5,2,32,128]{3,2,1,0:T(8,128)(2,1)S(1)} %get-tuple-element.9.refs_1_), channel_id=1, source_target_pairs={{0,16},{8,24},{16,0},{24,8},{1,17},{9,25},{17,1},{25,9},{2,18},{10... | collective-permute-start | bytes 245768 | tf_op jit(solution)/shard_map/ppermute | solution.py:287
  20.4 0.0 collective-permute-start.5
  20.4 0.5 %collective-permute-start.7 = (bf16[5,2,32,128]{3,2,1,0:T(8,128)(2,1)S(1)}, bf16[5,2,32,128]{3,2,1,0:T(8,128)(2,1)S(1)}, u32[]{:S(2)}, u32[]{:S(2)}) collective-permute-start(bf16[5,2,32,128]{3,2,1,0:T(8,128)(2,1)S(1)} %get-tuple-element.9.refs_1_), channel_id=1, source_target_pairs={{0,8},{8,0},{16,24},{24,16},{1,9},{9,1},{17,25},{25,17},{2,10},{10... | collective-permute-start | bytes 245768 | tf_op jit(solution)/shard_map/ppermute | solution.py:293
  20.9 2.4 %collective-permute-done.6.refs_2_ = bf16[5,2,32,128]{3,2,1,0:T(8,128)(2,1)S(1)} collective-permute-done((bf16[5,2,32,128]{3,2,1,0:T(8,128)(2,1)S(1)}, bf16[5,2,32,128]{3,2,1,0:T(8,128)(2,1)S(1)}, u32[]{:S(2)}, u32[]{:S(2)}) %collective-permute-start.6) | collective-permute-done | bytes 81952 | tf_op jit(solution)/shard_map/ppermute | solution.py:287
  23.3 0.0 collective-permute-start.8
  23.3 0.0 copy-start.1
  23.3 1.0 %copy-done.1 = bf16[512,512]{1,0:T(8,128)(2,1)S(1)} copy-done((bf16[512,512]{1,0:T(8,128)(2,1)S(1)}, bf16[512,512]{1,0:T(8,128)(2,1)}, u32[]{:S(2)}) %copy-start.1) | copy-done | bytes 524312
  24.4 0.2 turn.1
  24.6 0.0 collective-permute-done.5.refs_3_
  24.6 0.8 %prep.1.refs_0_ = bf16[8,6,64,128]{3,2,1,0:T(8,128)(2,1)S(1)} custom-call(s32[1]{0:T(128)} %bitcast.4.scalars, bf16[7,32,128]{2,1,0:T(8,128)(2,1)S(1)} %pad_maximum_fusion.1.own, bf16[7,32,128]{2,1,0:T(8,128)(2,1)S(1)} %collective-permute-done.opposite, bf16[13,32,128]{2,1,0:T(8,128)(2,1)S(1)} %collective-permute-done.2.refs_0_, ...), custom_call_target="tpu_custom_call" | custom-call | flops 100663296 | bytes 1572864 | tf_op jit(solution)/shard_map/prep/pallas_call | solution.py:321
  25.4 0.0 collective-permute-done.7.refs_3_
  25.4 0.0 collective-permute-done.8.refs_4_
  25.4 5.7 %tiles.1 = (bf16[6,64,512]{2,1,0:T(8,128)(2,1)}, bf16[6,512,512]{2,1,0:T(8,128)(2,1)}) custom-call(s32[1]{0:T(128)} %bitcast.2.places, s32[1]{0:T(128)} %bitcast.3.aways, bf16[8,6,64,128]{3,2,1,0:T(8,128)(2,1)S(1)} %prep.1.refs_0_, bf16[5,2,32,128]{3,2,1,0:T(8,128)(2,1)S(1)} %get-tuple-element.9.refs_1_, ...), custom_call_target="tpu_custom_call" | custom-call | tf_op jit(solution)/shard_map/tiles/pallas_call | solution.py:326
  (5 shorter events, 0.1 us)
Async XLA Ops:
  0.6 0.9 %copy-start = (bf16[12,1,64,64]{3,2,1,0:T(8,128)(2,1)S(1)}, bf16[12,1,64,64]{3,2,1,0:T(8,128)(2,1)}, u32[]{:S(2)}) copy-start(bf16[12,1,64,64]{3,2,1,0:T(8,128)(2,1)} %param.4) | copy-start | bytes 294916
  1.7 1.4 %collective-permute-start.1 = (bf16[7,32,128]{2,1,0:T(8,128)(2,1)S(1)}, bf16[7,32,128]{2,1,0:T(8,128)(2,1)S(1)}, u32[]{:S(2)}, u32[]{:S(2)}) collective-permute-start(bf16[7,32,128]{2,1,0:T(8,128)(2,1)S(1)} %pad_maximum_fusion.1.own), channel_id=1, source_target_pairs={{0,8},{8,0},{16,24},{24,16},{1,9},{9,1},{17,25},{25,17},{2,10},{10... | collective-permute-start | bytes 172040 | tf_op jit(solution)/shard_map/ppermute | solution.py:251
  3.3 14.8 %collective-permute-start.4 = (bf16[13,32,128]{2,1,0:T(8,128)(2,1)S(1)}, bf16[13,32,128]{2,1,0:T(8,128)(2,1)S(1)}, u32[]{:S(2)}, u32[]{:S(2)}) collective-permute-start(bf16[13,32,128]{2,1,0:T(8,128)(2,1)S(1)} %pad_maximum_fusion), channel_id=1, source_target_pairs={{0,6},{1,7},{2,4},{3,5},{4,2},{5,3},{6,0},{7,1},{8,9},{9,8},{10,11... | collective-permute-start | bytes 319496 | tf_op jit(solution)/shard_map/ppermute | solution.py:262
  8.3 10.5 %collective-permute-start.3 = (bf16[13,32,128]{2,1,0:T(8,128)(2,1)S(1)}, bf16[13,32,128]{2,1,0:T(8,128)(2,1)S(1)}, u32[]{:S(2)}, u32[]{:S(2)}) collective-permute-start(bf16[13,32,128]{2,1,0:T(8,128)(2,1)S(1)} %pad_maximum_fusion), channel_id=1, source_target_pairs={{0,5},{1,4},{2,7},{3,6},{4,1},{5,0},{6,3},{7,2},{8,10},{9,11},{10,... | collective-permute-start | bytes 319496 | tf_op jit(solution)/shard_map/ppermute | solution.py:262
  8.7 10.2 %collective-permute-start.2 = (bf16[13,32,128]{2,1,0:T(8,128)(2,1)S(1)}, bf16[13,32,128]{2,1,0:T(8,128)(2,1)S(1)}, u32[]{:S(2)}, u32[]{:S(2)}) collective-permute-start(bf16[13,32,128]{2,1,0:T(8,128)(2,1)S(1)} %pad_maximum_fusion), channel_id=1, source_target_pairs={{0,3},{1,2},{2,1},{3,0},{4,7},{5,6},{6,5},{7,4},{8,12},{9,13},{10,... | collective-permute-start | bytes 319496 | tf_op jit(solution)/shard_map/ppermute | solution.py:262
  9.8 8.2 %collective-permute-start = (bf16[7,32,128]{2,1,0:T(8,128)(2,1)S(1)}, bf16[7,32,128]{2,1,0:T(8,128)(2,1)S(1)}, u32[]{:S(2)}, u32[]{:S(2)}) collective-permute-start(bf16[7,32,128]{2,1,0:T(8,128)(2,1)S(1)} %pad_maximum_fusion.1.own), channel_id=1, source_target_pairs={{0,7},{1,6},{2,5},{3,4},{4,3},{5,2},{6,1},{7,0},{8,15},{9,14},{10,... | collective-permute-start | bytes 172040 | tf_op jit(solution)/shard_map/ppermute | solution.py:252
  18.8 4.5 %collective-permute-start.6 = (bf16[5,2,32,128]{3,2,1,0:T(8,128)(2,1)S(1)}, bf16[5,2,32,128]{3,2,1,0:T(8,128)(2,1)S(1)}, u32[]{:S(2)}, u32[]{:S(2)}) collective-permute-start(bf16[5,2,32,128]{3,2,1,0:T(8,128)(2,1)S(1)} %get-tuple-element.9.refs_1_), channel_id=1, source_target_pairs={{0,16},{8,24},{16,0},{24,8},{1,17},{9,25},{17,1},{25,9},{2,18},{10... | collective-permute-start | bytes 245768 | tf_op jit(solution)/shard_map/ppermute | solution.py:287
  20.4 4.2 %collective-permute-start.5 = (bf16[3,6,32,128]{3,2,1,0:T(8,128)(2,1)S(1)}, bf16[3,6,32,128]{3,2,1,0:T(8,128)(2,1)S(1)}, u32[]{:S(2)}, u32[]{:S(2)}) collective-permute-start(bf16[3,6,32,128]{3,2,1,0:T(8,128)(2,1)S(1)} %get-tuple-element.8), channel_id=1, source_target_pairs={{0,8},{8,0},{16,24},{24,16},{1,9},{9,1},{17,25},{25,17},{2,10},{10... | collective-permute-start | bytes 442376 | tf_op jit(solution)/shard_map/ppermute | solution.py:292
  20.4 5.0 %collective-permute-start.7 = (bf16[5,2,32,128]{3,2,1,0:T(8,128)(2,1)S(1)}, bf16[5,2,32,128]{3,2,1,0:T(8,128)(2,1)S(1)}, u32[]{:S(2)}, u32[]{:S(2)}) collective-permute-start(bf16[5,2,32,128]{3,2,1,0:T(8,128)(2,1)S(1)} %get-tuple-element.9.refs_1_), channel_id=1, source_target_pairs={{0,8},{8,0},{16,24},{24,16},{1,9},{9,1},{17,25},{25,17},{2,10},{10... | collective-permute-start | bytes 245768 | tf_op jit(solution)/shard_map/ppermute | solution.py:293
  23.3 2.1 %collective-permute-start.8 = (bf16[5,2,32,128]{3,2,1,0:T(8,128)(2,1)S(1)}, bf16[5,2,32,128]{3,2,1,0:T(8,128)(2,1)S(1)}, u32[]{:S(2)}, u32[]{:S(2)}) collective-permute-start(bf16[5,2,32,128]{3,2,1,0:T(8,128)(2,1)S(1)} %collective-permute-done.6.refs_2_), channel_id=1, source_target_pairs={{0,8},{8,0},{16,24},{24,16},{1,9},{9,1},{17,25},{25,17},{2,10},{10... | collective-permute-start | bytes 245768 | tf_op jit(solution)/shard_map/ppermute | solution.py:293
  23.3 1.0 %copy-start.1 = (bf16[512,512]{1,0:T(8,128)(2,1)S(1)}, bf16[512,512]{1,0:T(8,128)(2,1)}, u32[]{:S(2)}) copy-start(bf16[512,512]{1,0:T(8,128)(2,1)} %factor.1) | copy-start | bytes 1572868

commit v4 on v3

--- a/solution.py
+++ b/solution.py
@@ -102,7 +102,9 @@
     for packed, at in blocks:
         packed = packed.reshape(RW * half, width)
         for part, norm in enumerate(half_norms(packed, fold, dim)):
-            rows = with_norms(packed[:, part * dim : (part + 1) * dim], norm, dim)
+            points = packed[:, part * dim : (part + 1) * dim]
+            points = (points.astype(jnp.float32) / dim).astype(jnp.bfloat16)
+            rows = with_norms(points, norm * (1.0 / dim), dim)
             left[at, :, part * half : (part + 1) * half, :] = rows.reshape(RW, half, LANES)
 
 
@@ -122,7 +124,7 @@
     scale = 1.0 / dim
 
     tail = jnp.where(
-        lax.broadcasted_iota(jnp.int32, (half, LANES - dim), 1) < PIECES, -scale, 0.0
+        lax.broadcasted_iota(jnp.int32, (half, LANES - dim), 1) < PIECES, -1.0, 0.0
     ).astype(jnp.bfloat16)
 
     def from_row(lists, i, which):
@@ -143,23 +145,22 @@
             near, far = from_row(held, i, which), from_row(flipped, i, which)
             blocks.append((jnp.where(away[which] & 1 > 0, far, near), distance))
         for block, distance in blocks:
-            block = (block.astype(jnp.float32) * scale).astype(jnp.bfloat16)
             for part in range(fold):
                 start = pl.multiple_of((col_here ^ distance) * share + part * half, half)
                 points = block[:, part * dim : (part + 1) * dim]
                 right[pl.ds(start, half), :] = jnp.concatenate([points, tail], axis=1)
 
     lane = lax.broadcasted_iota(jnp.int32, (8, 2 * LANES), 1) % LANES
-    weight = jnp.where(lane < dim, dim / 2.0, 0.0).astype(jnp.bfloat16)
+    weight = jnp.where(lane < dim, 0.5 * scale, 0.0).astype(jnp.bfloat16)
     squares_j = split_squares(right_j[...])
     norm_p = dot(weight, split_squares(right_p[...]), NT)[:1]
     norm_j = dot(weight, squares_j, NT)[:1]
     lane = lax.broadcasted_iota(jnp.int32, (2 * LANES, LANES), 0) % LANES
-    weight = jnp.where(lane < dim, dim / 2.0, 0.0).astype(jnp.bfloat16)
+    weight = jnp.where(lane < dim, 0.5 * scale, 0.0).astype(jnp.bfloat16)
     rows_j = dot(squares_j, weight, NN)[:, :1]
 
     lane = lax.broadcasted_iota(jnp.int32, (side, LANES), 1)
-    bare_j = jnp.where(lane < dim, right_j[...].astype(jnp.float32) * dim, 0.0).astype(jnp.bfloat16)
+    bare_j = jnp.where(lane < dim, right_j[...].astype(jnp.float32) * scale, 0.0).astype(jnp.bfloat16)
     kjp = jnp.exp(dot(bare_j, right_p[...], NT) - rows_j - norm_p).astype(jnp.bfloat16)
 
     def by_factor(values):
@@ -192,6 +193,15 @@
             )
         ]
 
+    def last_copy(piece):
+        lines = pl.ds(piece * RW // 3, RW // 3)
+        row0 = pl.multiple_of((col_here ^ (peers - 1)) * share, share)
+        return pltpu.make_async_copy(
+            obuf.at[peers - 1, lines],
+            update_out.at[lines, pl.ds(row0, share), :],
+            sem.at[peers - 1, piece],
+        )
+
     def finish(step):
         slot = step % 2
         result = (ent[slot] - dot(kip[slot], mat[...], NN)).astype(jnp.bfloat16)
@@ -212,11 +222,20 @@
         kernels(step + 1)
         finish(step)
 
-    finish(steps - 1)
+    last = steps - 1
+    pieces = 3
+    for piece in range(pieces):
+        lines = slice(piece * RW // pieces, (piece + 1) * RW // pieces)
+        at = slice(lines.start * share, lines.stop * share)
+        result = ent[last % 2, at] - dot(kip[last % 2, at], mat[...], NN)
+        obuf[last, lines] = result.astype(jnp.bfloat16).reshape(-1, share, side)
+        last_copy(piece).start()
     panel_copy.wait()
-    for step in range(steps):
+    for step in range(steps - 1):
         for copy in out_copies(step):
             copy.wait()
+    for piece in range(pieces):
+        last_copy(piece).wait()
 
 
 def step(points, inverse_factor, panel_index, column_map):
@@ -244,7 +263,8 @@
         [local_points[:, part * half : (part + 1) * half] for part in range(fold)], axis=-1
     )
     across = col_count - 1
-    distances = [d for d in range(1, across) if d.bit_count() % 2 == 0]
+    middle = col_count // 2
+    distances = [2, across - 1, *range(3, middle)] if middle > 3 else list(range(1, middle))
     count = len(distances)
     core = row_here & 1
     flip = [(r, r ^ 1) for r in range(row_count)]
@@ -290,7 +310,9 @@
         bit >>= 1
     sources = [sources[source] for source in range(0, row_count, 2)]
     windows = lax.ppermute(windows, "row", flip)
-    flipped = [lax.ppermute(source, "row", flip) for source in sources]
+    flipped = []
+    for source in sources:
+        flipped.append(lax.ppermute(source, "row", flip))
 
     turn = pl.pallas_call(
         turn_kernel,

time: 31.3 us -> 30.1 us (0.962)
  starting transfers between devices: 13.9 us -> 10.6 us
  waiting for transfers between devices: 6.82 us -> 8.76 us
    ppermute x1, starting transfers between devices: 4.7 us -> 0.84 us  [step(): lax.ppermute(packed, 'col', [(c, c ^ across) for c in range(col_count)])]
    ppermute x1, waiting for transfers between devices: 2.78 us -> 5.34 us  [step(): lax.ppermute(packed, 'col', [(c, c ^ across) for c in range(col_count)])]
    ppermute x3, waiting for transfers between devices: 0.8 us -> 0.01 us  [step(): held[i] = lax.ppermute(mine, ('row', 'col'), pairs)]
    ppermute x3, starting transfers between devices: 6.54 us -> 7.08 us  [step(): held[i] = lax.ppermute(mine, ('row', 'col'), pairs)]
  transfers between devices with their start and end apart: 9 -> 9, of which waited for: 4 -> 3; matrix products, arithmetic and copies ran while one was open for 0% -> 0% of each run, Pallas kernels for 3% -> 4%
where the time goes in v4:
time: 30.1 us; the launch traced here: 29.8 us
  starting transfers between devices  10.6 us (35%)
  waiting for transfers between devices  8.76 us (29%)
  Pallas kernels  6.72 us (22%)
  between operations  2.17 us (7%)
  local copies, waits for them, and re-layouts  1.29 us (4%)
    ppermute x3, starting transfers between devices, step(): held[i] = lax.ppermute(mine, ('row', 'col'), pairs)  7.08 us
    pallas_call x1, Pallas kernels, step(): pl.pallas_call(functools.partial(main_kernel, peers, row_count // 2, fold...  5.65 us
    ppermute x1, waiting for transfers between devices, step(): lax.ppermute(packed, 'col', [(c, c ^ across) for c in range(col_count)])  5.34 us
    ppermute x1, waiting for transfers between devices, step(): lax.ppermute(sources[source], 'row', [(r, r ^ bit) for r in range(row_cou...  2.6 us
    ppermute x1, starting transfers between devices, step(): lax.ppermute(sources[source], 'row', [(r, r ^ bit) for r in range(row_cou...  1.56 us
    unnamed x4, local copies, waits for them, and re-layouts  1.26 us
    pallas_call x1, Pallas kernels, step(): left = prep(core[None].astype(jnp.int32), packed, opposite, *held, windows)  0.87 us
    ppermute x1, starting transfers between devices, step(): lax.ppermute(packed, 'col', [(c, c ^ across) for c in range(col_count)])  0.84 us
  transfers between devices with their start and end apart: 9, of which 3 were waited for; matrix products, arithmetic and copies ran while one was open for 0% of the time, Pallas kernels for 4%

profile of v4, /device:TPU:0, one launch (start us, length us, event | category | flops | bytes accessed | tf_op | source)
XLA Modules:
  0.0 29.8 jit_solution(16286724823575019149)
XLA Ops:
  0.6 0.0 copy-start
  1.4 0.2 copy-done
  1.6 0.1 pad_maximum_fusion.1.own
  1.7 0.6 %collective-permute-start.1 = (bf16[7,32,128]{2,1,0:T(8,128)(2,1)S(1)}, bf16[7,32,128]{2,1,0:T(8,128)(2,1)S(1)}, u32[]{:S(2)}, u32[]{:S(2)}) collective-permute-start(bf16[7,32,128]{2,1,0:T(8,128)(2,1)S(1)} %pad_maximum_fusion.1.own), channel_id=1, source_target_pairs={{0,8},{8,0},{16,24},{24,16},{1,9},{9,1},{17,25},{25,17},{2,10},{10... | collective-permute-start | bytes 172040 | tf_op jit(solution)/shard_map/ppermute | solution.py:271
  2.3 0.1 slice_maximum_fusion
  2.4 0.8 %collective-permute-done.1 = bf16[7,32,128]{2,1,0:T(8,128)(2,1)S(1)} collective-permute-done((bf16[7,32,128]{2,1,0:T(8,128)(2,1)S(1)}, bf16[7,32,128]{2,1,0:T(8,128)(2,1)S(1)}, u32[]{:S(2)}, u32[]{:S(2)}) %collective-permute-start.1) | collective-permute-done | bytes 57376 | tf_op jit(solution)/shard_map/ppermute | solution.py:271
  3.2 0.1 fusion.1
  3.3 3.9 %collective-permute-start.4 = (bf16[13,32,128]{2,1,0:T(8,128)(2,1)S(1)}, bf16[13,32,128]{2,1,0:T(8,128)(2,1)S(1)}, u32[]{:S(2)}, u32[]{:S(2)}) collective-permute-start(bf16[13,32,128]{2,1,0:T(8,128)(2,1)S(1)} %pad_maximum_fusion), channel_id=1, source_target_pairs={{0,3},{1,2},{2,1},{3,0},{4,7},{5,6},{6,5},{7,4},{8,12},{9,13},{10,... | collective-permute-start | bytes 319496 | tf_op jit(solution)/shard_map/ppermute | solution.py:282
  7.2 2.5 %collective-permute-start.3 = (bf16[13,32,128]{2,1,0:T(8,128)(2,1)S(1)}, bf16[13,32,128]{2,1,0:T(8,128)(2,1)S(1)}, u32[]{:S(2)}, u32[]{:S(2)}) collective-permute-start(bf16[13,32,128]{2,1,0:T(8,128)(2,1)S(1)} %pad_maximum_fusion), channel_id=1, source_target_pairs={{0,6},{1,7},{2,4},{3,5},{4,2},{5,3},{6,0},{7,1},{8,9},{9,8},{10,11... | collective-permute-start | bytes 319496 | tf_op jit(solution)/shard_map/ppermute | solution.py:282
  9.7 0.7 %collective-permute-start.2 = (bf16[13,32,128]{2,1,0:T(8,128)(2,1)S(1)}, bf16[13,32,128]{2,1,0:T(8,128)(2,1)S(1)}, u32[]{:S(2)}, u32[]{:S(2)}) collective-permute-start(bf16[13,32,128]{2,1,0:T(8,128)(2,1)S(1)} %pad_maximum_fusion), channel_id=1, source_target_pairs={{0,2},{1,3},{2,0},{3,1},{4,6},{5,7},{6,4},{7,5},{8,13},{9,12},{10,... | collective-permute-start | bytes 319496 | tf_op jit(solution)/shard_map/ppermute | solution.py:282
  10.3 0.8 %collective-permute-start = (bf16[7,32,128]{2,1,0:T(8,128)(2,1)S(1)}, bf16[7,32,128]{2,1,0:T(8,128)(2,1)S(1)}, u32[]{:S(2)}, u32[]{:S(2)}) collective-permute-start(bf16[7,32,128]{2,1,0:T(8,128)(2,1)S(1)} %pad_maximum_fusion.1.own), channel_id=1, source_target_pairs={{0,7},{1,6},{2,5},{3,4},{4,3},{5,2},{6,1},{7,0},{8,15},{9,14},{10,... | collective-permute-start | bytes 172040 | tf_op jit(solution)/shard_map/ppermute | solution.py:272
  11.9 5.3 %collective-permute-done.opposite = bf16[7,32,128]{2,1,0:T(8,128)(2,1)S(1)} collective-permute-done((bf16[7,32,128]{2,1,0:T(8,128)(2,1)S(1)}, bf16[7,32,128]{2,1,0:T(8,128)(2,1)S(1)}, u32[]{:S(2)}, u32[]{:S(2)}) %collective-permute-start) | collective-permute-done | bytes 57376 | tf_op jit(solution)/shard_map/ppermute | solution.py:272
  17.3 0.0 collective-permute-done.4.refs_2_
  17.3 0.0 collective-permute-done.3.refs_1_
  17.3 0.0 collective-permute-done.2.refs_0_
  17.3 1.6 %collective-permute-start.6 = (bf16[5,2,32,128]{3,2,1,0:T(8,128)(2,1)S(1)}, bf16[5,2,32,128]{3,2,1,0:T(8,128)(2,1)S(1)}, u32[]{:S(2)}, u32[]{:S(2)}) collective-permute-start(bf16[5,2,32,128]{3,2,1,0:T(8,128)(2,1)S(1)} %get-tuple-element.9.refs_1_), channel_id=1, source_target_pairs={{0,16},{8,24},{16,0},{24,8},{1,17},{9,25},{17,1},{25,9},{2,18},{10... | collective-permute-start | bytes 245768 | tf_op jit(solution)/shard_map/ppermute | solution.py:307
  18.9 0.0 collective-permute-start.5
  18.9 0.5 %collective-permute-start.7 = (bf16[5,2,32,128]{3,2,1,0:T(8,128)(2,1)S(1)}, bf16[5,2,32,128]{3,2,1,0:T(8,128)(2,1)S(1)}, u32[]{:S(2)}, u32[]{:S(2)}) collective-permute-start(bf16[5,2,32,128]{3,2,1,0:T(8,128)(2,1)S(1)} %get-tuple-element.9.refs_1_), channel_id=1, source_target_pairs={{0,8},{8,0},{16,24},{24,16},{1,9},{9,1},{17,25},{25,17},{2,10},{10... | collective-permute-start | bytes 245768 | tf_op jit(solution)/shard_map/ppermute | solution.py:315
  19.4 2.6 %collective-permute-done.6.refs_2_ = bf16[5,2,32,128]{3,2,1,0:T(8,128)(2,1)S(1)} collective-permute-done((bf16[5,2,32,128]{3,2,1,0:T(8,128)(2,1)S(1)}, bf16[5,2,32,128]{3,2,1,0:T(8,128)(2,1)S(1)}, u32[]{:S(2)}, u32[]{:S(2)}) %collective-permute-start.6) | collective-permute-done | bytes 81952 | tf_op jit(solution)/shard_map/ppermute | solution.py:307
  22.0 0.0 collective-permute-start.8
  22.0 0.0 copy-start.1
  22.0 1.0 %copy-done.1 = bf16[512,512]{1,0:T(8,128)(2,1)S(1)} copy-done((bf16[512,512]{1,0:T(8,128)(2,1)S(1)}, bf16[512,512]{1,0:T(8,128)(2,1)}, u32[]{:S(2)}) %copy-start.1) | copy-done | bytes 524312
  23.0 0.2 turn.1
  23.2 0.0 collective-permute-done.5.refs_3_
  23.2 0.9 %prep.1.refs_0_ = bf16[8,6,64,128]{3,2,1,0:T(8,128)(2,1)S(1)} custom-call(s32[1]{0:T(128)} %bitcast.4.scalars, bf16[7,32,128]{2,1,0:T(8,128)(2,1)S(1)} %pad_maximum_fusion.1.own, bf16[7,32,128]{2,1,0:T(8,128)(2,1)S(1)} %collective-permute-done.opposite, bf16[13,32,128]{2,1,0:T(8,128)(2,1)S(1)} %collective-permute-done.2.refs_0_, ...), custom_call_target="tpu_custom_call" | custom-call | flops 100663296 | bytes 1572864 | tf_op jit(solution)/shard_map/prep/pallas_call | solution.py:343
  24.1 0.0 collective-permute-done.7.refs_3_
  24.1 0.0 collective-permute-done.8.refs_4_
  24.1 5.6 %tiles.1 = (bf16[6,64,512]{2,1,0:T(8,128)(2,1)}, bf16[6,512,512]{2,1,0:T(8,128)(2,1)}) custom-call(s32[1]{0:T(128)} %bitcast.2.places, s32[1]{0:T(128)} %bitcast.3.aways, bf16[8,6,64,128]{3,2,1,0:T(8,128)(2,1)S(1)} %prep.1.refs_0_, bf16[5,2,32,128]{3,2,1,0:T(8,128)(2,1)S(1)} %get-tuple-element.9.refs_1_, ...), custom_call_target="tpu_custom_call" | custom-call | tf_op jit(solution)/shard_map/tiles/pallas_call | solution.py:348
  (5 shorter events, 0.1 us)
Async XLA Ops:
  0.6 0.9 %copy-start = (bf16[12,1,64,64]{3,2,1,0:T(8,128)(2,1)S(1)}, bf16[12,1,64,64]{3,2,1,0:T(8,128)(2,1)}, u32[]{:S(2)}) copy-start(bf16[12,1,64,64]{3,2,1,0:T(8,128)(2,1)} %param.4) | copy-start | bytes 294916
  1.7 1.4 %collective-permute-start.1 = (bf16[7,32,128]{2,1,0:T(8,128)(2,1)S(1)}, bf16[7,32,128]{2,1,0:T(8,128)(2,1)S(1)}, u32[]{:S(2)}, u32[]{:S(2)}) collective-permute-start(bf16[7,32,128]{2,1,0:T(8,128)(2,1)S(1)} %pad_maximum_fusion.1.own), channel_id=1, source_target_pairs={{0,8},{8,0},{16,24},{24,16},{1,9},{9,1},{17,25},{25,17},{2,10},{10... | collective-permute-start | bytes 172040 | tf_op jit(solution)/shard_map/ppermute | solution.py:271
  3.3 14.0 %collective-permute-start.4 = (bf16[13,32,128]{2,1,0:T(8,128)(2,1)S(1)}, bf16[13,32,128]{2,1,0:T(8,128)(2,1)S(1)}, u32[]{:S(2)}, u32[]{:S(2)}) collective-permute-start(bf16[13,32,128]{2,1,0:T(8,128)(2,1)S(1)} %pad_maximum_fusion), channel_id=1, source_target_pairs={{0,3},{1,2},{2,1},{3,0},{4,7},{5,6},{6,5},{7,4},{8,12},{9,13},{10,... | collective-permute-start | bytes 319496 | tf_op jit(solution)/shard_map/ppermute | solution.py:282
  7.2 10.1 %collective-permute-start.3 = (bf16[13,32,128]{2,1,0:T(8,128)(2,1)S(1)}, bf16[13,32,128]{2,1,0:T(8,128)(2,1)S(1)}, u32[]{:S(2)}, u32[]{:S(2)}) collective-permute-start(bf16[13,32,128]{2,1,0:T(8,128)(2,1)S(1)} %pad_maximum_fusion), channel_id=1, source_target_pairs={{0,6},{1,7},{2,4},{3,5},{4,2},{5,3},{6,0},{7,1},{8,9},{9,8},{10,11... | collective-permute-start | bytes 319496 | tf_op jit(solution)/shard_map/ppermute | solution.py:282
  9.7 7.6 %collective-permute-start.2 = (bf16[13,32,128]{2,1,0:T(8,128)(2,1)S(1)}, bf16[13,32,128]{2,1,0:T(8,128)(2,1)S(1)}, u32[]{:S(2)}, u32[]{:S(2)}) collective-permute-start(bf16[13,32,128]{2,1,0:T(8,128)(2,1)S(1)} %pad_maximum_fusion), channel_id=1, source_target_pairs={{0,2},{1,3},{2,0},{3,1},{4,6},{5,7},{6,4},{7,5},{8,13},{9,12},{10,... | collective-permute-start | bytes 319496 | tf_op jit(solution)/shard_map/ppermute | solution.py:282
  10.3 6.9 %collective-permute-start = (bf16[7,32,128]{2,1,0:T(8,128)(2,1)S(1)}, bf16[7,32,128]{2,1,0:T(8,128)(2,1)S(1)}, u32[]{:S(2)}, u32[]{:S(2)}) collective-permute-start(bf16[7,32,128]{2,1,0:T(8,128)(2,1)S(1)} %pad_maximum_fusion.1.own), channel_id=1, source_target_pairs={{0,7},{1,6},{2,5},{3,4},{4,3},{5,2},{6,1},{7,0},{8,15},{9,14},{10,... | collective-permute-start | bytes 172040 | tf_op jit(solution)/shard_map/ppermute | solution.py:272
  17.3 4.7 %collective-permute-start.6 = (bf16[5,2,32,128]{3,2,1,0:T(8,128)(2,1)S(1)}, bf16[5,2,32,128]{3,2,1,0:T(8,128)(2,1)S(1)}, u32[]{:S(2)}, u32[]{:S(2)}) collective-permute-start(bf16[5,2,32,128]{3,2,1,0:T(8,128)(2,1)S(1)} %get-tuple-element.9.refs_1_), channel_id=1, source_target_pairs={{0,16},{8,24},{16,0},{24,8},{1,17},{9,25},{17,1},{25,9},{2,18},{10... | collective-permute-start | bytes 245768 | tf_op jit(solution)/shard_map/ppermute | solution.py:307
  18.9 4.4 %collective-permute-start.5 = (bf16[3,6,32,128]{3,2,1,0:T(8,128)(2,1)S(1)}, bf16[3,6,32,128]{3,2,1,0:T(8,128)(2,1)S(1)}, u32[]{:S(2)}, u32[]{:S(2)}) collective-permute-start(bf16[3,6,32,128]{3,2,1,0:T(8,128)(2,1)S(1)} %get-tuple-element.8), channel_id=1, source_target_pairs={{0,8},{8,0},{16,24},{24,16},{1,9},{9,1},{17,25},{25,17},{2,10},{10... | collective-permute-start | bytes 442376 | tf_op jit(solution)/shard_map/ppermute | solution.py:312
  18.9 5.2 %collective-permute-start.7 = (bf16[5,2,32,128]{3,2,1,0:T(8,128)(2,1)S(1)}, bf16[5,2,32,128]{3,2,1,0:T(8,128)(2,1)S(1)}, u32[]{:S(2)}, u32[]{:S(2)}) collective-permute-start(bf16[5,2,32,128]{3,2,1,0:T(8,128)(2,1)S(1)} %get-tuple-element.9.refs_1_), channel_id=1, source_target_pairs={{0,8},{8,0},{16,24},{24,16},{1,9},{9,1},{17,25},{25,17},{2,10},{10... | collective-permute-start | bytes 245768 | tf_op jit(solution)/shard_map/ppermute | solution.py:315
  22.0 2.1 %collective-permute-start.8 = (bf16[5,2,32,128]{3,2,1,0:T(8,128)(2,1)S(1)}, bf16[5,2,32,128]{3,2,1,0:T(8,128)(2,1)S(1)}, u32[]{:S(2)}, u32[]{:S(2)}) collective-permute-start(bf16[5,2,32,128]{3,2,1,0:T(8,128)(2,1)S(1)} %collective-permute-done.6.refs_2_), channel_id=1, source_target_pairs={{0,8},{8,0},{16,24},{24,16},{1,9},{9,1},{17,25},{25,17},{2,10},{10... | collective-permute-start | bytes 245768 | tf_op jit(solution)/shard_map/ppermute | solution.py:315
  22.0 1.0 %copy-start.1 = (bf16[512,512]{1,0:T(8,128)(2,1)S(1)}, bf16[512,512]{1,0:T(8,128)(2,1)}, u32[]{:S(2)}) copy-start(bf16[512,512]{1,0:T(8,128)(2,1)} %factor.1) | copy-start | bytes 1572868

commit v5 on v4

--- a/solution.py
+++ b/solution.py
@@ -60,6 +60,7 @@
 
 
 FIELD = 8
+GUARD = 2.0**48
 
 
 def packed_scalars(*values):
@@ -87,7 +88,7 @@
 
 def turn_kernel(factor, factor_copy, factor_t):
     factor_copy[...] = factor[...]
-    factor_t[...] = factor[...].T
+    factor_t[...] = (factor[...].T.astype(jnp.float32) / GUARD).astype(jnp.bfloat16)
 
 
 def prep_kernel(count, fold, dim, distances, scalars, own, opposite, *refs):
@@ -204,7 +205,7 @@
 
     def finish(step):
         slot = step % 2
-        result = (ent[slot] - dot(kip[slot], mat[...], NN)).astype(jnp.bfloat16)
+        result = (ent[slot] - dot(kip[slot], mat[...], NN) * GUARD).astype(jnp.bfloat16)
         obuf[step] = result.reshape(RW, share, side)
         for copy in out_copies(step):
             copy.start()
@@ -219,15 +220,15 @@
     panel_copy.start()
 
     for step in range(steps - 1):
+        finish(step)
         kernels(step + 1)
-        finish(step)
 
     last = steps - 1
     pieces = 3
     for piece in range(pieces):
         lines = slice(piece * RW // pieces, (piece + 1) * RW // pieces)
         at = slice(lines.start * share, lines.stop * share)
-        result = ent[last % 2, at] - dot(kip[last % 2, at], mat[...], NN)
+        result = ent[last % 2, at] - dot(kip[last % 2, at], mat[...], NN) * GUARD
         obuf[last, lines] = result.astype(jnp.bfloat16).reshape(-1, share, side)
         last_copy(piece).start()
     panel_copy.wait()

time: 30.1 us -> 30.1 us (level)
  no operation moved by 1% of the time
where the time goes in v5:
time: 30.1 us; the launch traced here: 29.8 us
  starting transfers between devices  10.6 us (35%)
  waiting for transfers between devices  8.76 us (29%)
  Pallas kernels  6.73 us (22%)
  between operations  2.17 us (7%)
  local copies, waits for them, and re-layouts  1.29 us (4%)
    ppermute x3, starting transfers between devices, step(): held[i] = lax.ppermute(mine, ('row', 'col'), pairs)  7.08 us
    pallas_call x1, Pallas kernels, step(): pl.pallas_call(functools.partial(main_kernel, peers, row_count // 2, fold...  5.65 us
    ppermute x1, waiting for transfers between devices, step(): lax.ppermute(packed, 'col', [(c, c ^ across) for c in range(col_count)])  5.34 us
    ppermute x1, waiting for transfers between devices, step(): lax.ppermute(sources[source], 'row', [(r, r ^ bit) for r in range(row_cou...  2.6 us
    ppermute x1, starting transfers between devices, step(): lax.ppermute(sources[source], 'row', [(r, r ^ bit) for r in range(row_cou...  1.56 us
    unnamed x4, local copies, waits for them, and re-layouts  1.26 us
    pallas_call x1, Pallas kernels, step(): left = prep(core[None].astype(jnp.int32), packed, opposite, *held, windows)  0.87 us
    ppermute x1, starting transfers between devices, step(): lax.ppermute(packed, 'col', [(c, c ^ across) for c in range(col_count)])  0.84 us
  transfers between devices with their start and end apart: 9, of which 3 were waited for; matrix products, arithmetic and copies ran while one was open for 0% of the time, Pallas kernels for 4%

profile of v5, /device:TPU:0, one launch (start us, length us, event | category | flops | bytes accessed | tf_op | source)
XLA Modules:
  0.0 29.8 jit_solution(10428549554414287099)
XLA Ops:
  0.6 0.0 copy-start
  1.4 0.2 copy-done
  1.6 0.1 pad_maximum_fusion.1.own
  1.7 0.6 %collective-permute-start.1 = (bf16[7,32,128]{2,1,0:T(8,128)(2,1)S(1)}, bf16[7,32,128]{2,1,0:T(8,128)(2,1)S(1)}, u32[]{:S(2)}, u32[]{:S(2)}) collective-permute-start(bf16[7,32,128]{2,1,0:T(8,128)(2,1)S(1)} %pad_maximum_fusion.1.own), channel_id=1, source_target_pairs={{0,8},{8,0},{16,24},{24,16},{1,9},{9,1},{17,25},{25,17},{2,10},{10... | collective-permute-start | bytes 172040 | tf_op jit(solution)/shard_map/ppermute | solution.py:272
  2.3 0.1 slice_maximum_fusion
  2.4 0.8 %collective-permute-done.1 = bf16[7,32,128]{2,1,0:T(8,128)(2,1)S(1)} collective-permute-done((bf16[7,32,128]{2,1,0:T(8,128)(2,1)S(1)}, bf16[7,32,128]{2,1,0:T(8,128)(2,1)S(1)}, u32[]{:S(2)}, u32[]{:S(2)}) %collective-permute-start.1) | collective-permute-done | bytes 57376 | tf_op jit(solution)/shard_map/ppermute | solution.py:272
  3.2 0.1 fusion.1
  3.3 3.9 %collective-permute-start.4 = (bf16[13,32,128]{2,1,0:T(8,128)(2,1)S(1)}, bf16[13,32,128]{2,1,0:T(8,128)(2,1)S(1)}, u32[]{:S(2)}, u32[]{:S(2)}) collective-permute-start(bf16[13,32,128]{2,1,0:T(8,128)(2,1)S(1)} %pad_maximum_fusion), channel_id=1, source_target_pairs={{0,3},{1,2},{2,1},{3,0},{4,7},{5,6},{6,5},{7,4},{8,12},{9,13},{10,... | collective-permute-start | bytes 319496 | tf_op jit(solution)/shard_map/ppermute | solution.py:283
  7.2 2.5 %collective-permute-start.3 = (bf16[13,32,128]{2,1,0:T(8,128)(2,1)S(1)}, bf16[13,32,128]{2,1,0:T(8,128)(2,1)S(1)}, u32[]{:S(2)}, u32[]{:S(2)}) collective-permute-start(bf16[13,32,128]{2,1,0:T(8,128)(2,1)S(1)} %pad_maximum_fusion), channel_id=1, source_target_pairs={{0,6},{1,7},{2,4},{3,5},{4,2},{5,3},{6,0},{7,1},{8,9},{9,8},{10,11... | collective-permute-start | bytes 319496 | tf_op jit(solution)/shard_map/ppermute | solution.py:283
  9.7 0.7 %collective-permute-start.2 = (bf16[13,32,128]{2,1,0:T(8,128)(2,1)S(1)}, bf16[13,32,128]{2,1,0:T(8,128)(2,1)S(1)}, u32[]{:S(2)}, u32[]{:S(2)}) collective-permute-start(bf16[13,32,128]{2,1,0:T(8,128)(2,1)S(1)} %pad_maximum_fusion), channel_id=1, source_target_pairs={{0,2},{1,3},{2,0},{3,1},{4,6},{5,7},{6,4},{7,5},{8,13},{9,12},{10,... | collective-permute-start | bytes 319496 | tf_op jit(solution)/shard_map/ppermute | solution.py:283
  10.3 0.8 %collective-permute-start = (bf16[7,32,128]{2,1,0:T(8,128)(2,1)S(1)}, bf16[7,32,128]{2,1,0:T(8,128)(2,1)S(1)}, u32[]{:S(2)}, u32[]{:S(2)}) collective-permute-start(bf16[7,32,128]{2,1,0:T(8,128)(2,1)S(1)} %pad_maximum_fusion.1.own), channel_id=1, source_target_pairs={{0,7},{1,6},{2,5},{3,4},{4,3},{5,2},{6,1},{7,0},{8,15},{9,14},{10,... | collective-permute-start | bytes 172040 | tf_op jit(solution)/shard_map/ppermute | solution.py:273
  11.9 5.3 %collective-permute-done.opposite = bf16[7,32,128]{2,1,0:T(8,128)(2,1)S(1)} collective-permute-done((bf16[7,32,128]{2,1,0:T(8,128)(2,1)S(1)}, bf16[7,32,128]{2,1,0:T(8,128)(2,1)S(1)}, u32[]{:S(2)}, u32[]{:S(2)}) %collective-permute-start) | collective-permute-done | bytes 57376 | tf_op jit(solution)/shard_map/ppermute | solution.py:273
  17.3 0.0 collective-permute-done.4.refs_2_
  17.3 0.0 collective-permute-done.3.refs_1_
  17.3 0.0 collective-permute-done.2.refs_0_
  17.3 1.6 %collective-permute-start.6 = (bf16[5,2,32,128]{3,2,1,0:T(8,128)(2,1)S(1)}, bf16[5,2,32,128]{3,2,1,0:T(8,128)(2,1)S(1)}, u32[]{:S(2)}, u32[]{:S(2)}) collective-permute-start(bf16[5,2,32,128]{3,2,1,0:T(8,128)(2,1)S(1)} %get-tuple-element.9.refs_1_), channel_id=1, source_target_pairs={{0,16},{8,24},{16,0},{24,8},{1,17},{9,25},{17,1},{25,9},{2,18},{10... | collective-permute-start | bytes 245768 | tf_op jit(solution)/shard_map/ppermute | solution.py:308
  18.9 0.0 collective-permute-start.5
  18.9 0.5 %collective-permute-start.7 = (bf16[5,2,32,128]{3,2,1,0:T(8,128)(2,1)S(1)}, bf16[5,2,32,128]{3,2,1,0:T(8,128)(2,1)S(1)}, u32[]{:S(2)}, u32[]{:S(2)}) collective-permute-start(bf16[5,2,32,128]{3,2,1,0:T(8,128)(2,1)S(1)} %get-tuple-element.9.refs_1_), channel_id=1, source_target_pairs={{0,8},{8,0},{16,24},{24,16},{1,9},{9,1},{17,25},{25,17},{2,10},{10... | collective-permute-start | bytes 245768 | tf_op jit(solution)/shard_map/ppermute | solution.py:316
  19.4 2.6 %collective-permute-done.6.refs_2_ = bf16[5,2,32,128]{3,2,1,0:T(8,128)(2,1)S(1)} collective-permute-done((bf16[5,2,32,128]{3,2,1,0:T(8,128)(2,1)S(1)}, bf16[5,2,32,128]{3,2,1,0:T(8,128)(2,1)S(1)}, u32[]{:S(2)}, u32[]{:S(2)}) %collective-permute-start.6) | collective-permute-done | bytes 81952 | tf_op jit(solution)/shard_map/ppermute | solution.py:308
  22.0 0.0 collective-permute-start.8
  22.0 0.0 copy-start.1
  22.0 1.0 %copy-done.1 = bf16[512,512]{1,0:T(8,128)(2,1)S(1)} copy-done((bf16[512,512]{1,0:T(8,128)(2,1)S(1)}, bf16[512,512]{1,0:T(8,128)(2,1)}, u32[]{:S(2)}) %copy-start.1) | copy-done | bytes 524312
  23.0 0.2 turn.1
  23.2 0.0 collective-permute-done.5.refs_3_
  23.2 0.9 %prep.1.refs_0_ = bf16[8,6,64,128]{3,2,1,0:T(8,128)(2,1)S(1)} custom-call(s32[1]{0:T(128)} %bitcast.4.scalars, bf16[7,32,128]{2,1,0:T(8,128)(2,1)S(1)} %pad_maximum_fusion.1.own, bf16[7,32,128]{2,1,0:T(8,128)(2,1)S(1)} %collective-permute-done.opposite, bf16[13,32,128]{2,1,0:T(8,128)(2,1)S(1)} %collective-permute-done.2.refs_0_, ...), custom_call_target="tpu_custom_call" | custom-call | flops 100663296 | bytes 1572864 | tf_op jit(solution)/shard_map/prep/pallas_call | solution.py:344
  24.1 0.0 collective-permute-done.7.refs_3_
  24.1 0.0 collective-permute-done.8.refs_4_
  24.1 5.6 %tiles.1 = (bf16[6,64,512]{2,1,0:T(8,128)(2,1)}, bf16[6,512,512]{2,1,0:T(8,128)(2,1)}) custom-call(s32[1]{0:T(128)} %bitcast.2.places, s32[1]{0:T(128)} %bitcast.3.aways, bf16[8,6,64,128]{3,2,1,0:T(8,128)(2,1)S(1)} %prep.1.refs_0_, bf16[5,2,32,128]{3,2,1,0:T(8,128)(2,1)S(1)} %get-tuple-element.9.refs_1_, ...), custom_call_target="tpu_custom_call" | custom-call | tf_op jit(solution)/shard_map/tiles/pallas_call | solution.py:349
  (5 shorter events, 0.1 us)
Async XLA Ops:
  0.6 0.9 %copy-start = (bf16[12,1,64,64]{3,2,1,0:T(8,128)(2,1)S(1)}, bf16[12,1,64,64]{3,2,1,0:T(8,128)(2,1)}, u32[]{:S(2)}) copy-start(bf16[12,1,64,64]{3,2,1,0:T(8,128)(2,1)} %param.4) | copy-start | bytes 294916
  1.7 1.4 %collective-permute-start.1 = (bf16[7,32,128]{2,1,0:T(8,128)(2,1)S(1)}, bf16[7,32,128]{2,1,0:T(8,128)(2,1)S(1)}, u32[]{:S(2)}, u32[]{:S(2)}) collective-permute-start(bf16[7,32,128]{2,1,0:T(8,128)(2,1)S(1)} %pad_maximum_fusion.1.own), channel_id=1, source_target_pairs={{0,8},{8,0},{16,24},{24,16},{1,9},{9,1},{17,25},{25,17},{2,10},{10... | collective-permute-start | bytes 172040 | tf_op jit(solution)/shard_map/ppermute | solution.py:272
  3.3 14.0 %collective-permute-start.4 = (bf16[13,32,128]{2,1,0:T(8,128)(2,1)S(1)}, bf16[13,32,128]{2,1,0:T(8,128)(2,1)S(1)}, u32[]{:S(2)}, u32[]{:S(2)}) collective-permute-start(bf16[13,32,128]{2,1,0:T(8,128)(2,1)S(1)} %pad_maximum_fusion), channel_id=1, source_target_pairs={{0,3},{1,2},{2,1},{3,0},{4,7},{5,6},{6,5},{7,4},{8,12},{9,13},{10,... | collective-permute-start | bytes 319496 | tf_op jit(solution)/shard_map/ppermute | solution.py:283
  7.2 10.1 %collective-permute-start.3 = (bf16[13,32,128]{2,1,0:T(8,128)(2,1)S(1)}, bf16[13,32,128]{2,1,0:T(8,128)(2,1)S(1)}, u32[]{:S(2)}, u32[]{:S(2)}) collective-permute-start(bf16[13,32,128]{2,1,0:T(8,128)(2,1)S(1)} %pad_maximum_fusion), channel_id=1, source_target_pairs={{0,6},{1,7},{2,4},{3,5},{4,2},{5,3},{6,0},{7,1},{8,9},{9,8},{10,11... | collective-permute-start | bytes 319496 | tf_op jit(solution)/shard_map/ppermute | solution.py:283
  9.7 7.6 %collective-permute-start.2 = (bf16[13,32,128]{2,1,0:T(8,128)(2,1)S(1)}, bf16[13,32,128]{2,1,0:T(8,128)(2,1)S(1)}, u32[]{:S(2)}, u32[]{:S(2)}) collective-permute-start(bf16[13,32,128]{2,1,0:T(8,128)(2,1)S(1)} %pad_maximum_fusion), channel_id=1, source_target_pairs={{0,2},{1,3},{2,0},{3,1},{4,6},{5,7},{6,4},{7,5},{8,13},{9,12},{10,... | collective-permute-start | bytes 319496 | tf_op jit(solution)/shard_map/ppermute | solution.py:283
  10.3 6.9 %collective-permute-start = (bf16[7,32,128]{2,1,0:T(8,128)(2,1)S(1)}, bf16[7,32,128]{2,1,0:T(8,128)(2,1)S(1)}, u32[]{:S(2)}, u32[]{:S(2)}) collective-permute-start(bf16[7,32,128]{2,1,0:T(8,128)(2,1)S(1)} %pad_maximum_fusion.1.own), channel_id=1, source_target_pairs={{0,7},{1,6},{2,5},{3,4},{4,3},{5,2},{6,1},{7,0},{8,15},{9,14},{10,... | collective-permute-start | bytes 172040 | tf_op jit(solution)/shard_map/ppermute | solution.py:273
  17.3 4.7 %collective-permute-start.6 = (bf16[5,2,32,128]{3,2,1,0:T(8,128)(2,1)S(1)}, bf16[5,2,32,128]{3,2,1,0:T(8,128)(2,1)S(1)}, u32[]{:S(2)}, u32[]{:S(2)}) collective-permute-start(bf16[5,2,32,128]{3,2,1,0:T(8,128)(2,1)S(1)} %get-tuple-element.9.refs_1_), channel_id=1, source_target_pairs={{0,16},{8,24},{16,0},{24,8},{1,17},{9,25},{17,1},{25,9},{2,18},{10... | collective-permute-start | bytes 245768 | tf_op jit(solution)/shard_map/ppermute | solution.py:308
  18.9 4.4 %collective-permute-start.5 = (bf16[3,6,32,128]{3,2,1,0:T(8,128)(2,1)S(1)}, bf16[3,6,32,128]{3,2,1,0:T(8,128)(2,1)S(1)}, u32[]{:S(2)}, u32[]{:S(2)}) collective-permute-start(bf16[3,6,32,128]{3,2,1,0:T(8,128)(2,1)S(1)} %get-tuple-element.8), channel_id=1, source_target_pairs={{0,8},{8,0},{16,24},{24,16},{1,9},{9,1},{17,25},{25,17},{2,10},{10... | collective-permute-start | bytes 442376 | tf_op jit(solution)/shard_map/ppermute | solution.py:313
  18.9 5.2 %collective-permute-start.7 = (bf16[5,2,32,128]{3,2,1,0:T(8,128)(2,1)S(1)}, bf16[5,2,32,128]{3,2,1,0:T(8,128)(2,1)S(1)}, u32[]{:S(2)}, u32[]{:S(2)}) collective-permute-start(bf16[5,2,32,128]{3,2,1,0:T(8,128)(2,1)S(1)} %get-tuple-element.9.refs_1_), channel_id=1, source_target_pairs={{0,8},{8,0},{16,24},{24,16},{1,9},{9,1},{17,25},{25,17},{2,10},{10... | collective-permute-start | bytes 245768 | tf_op jit(solution)/shard_map/ppermute | solution.py:316
  22.0 2.2 %collective-permute-start.8 = (bf16[5,2,32,128]{3,2,1,0:T(8,128)(2,1)S(1)}, bf16[5,2,32,128]{3,2,1,0:T(8,128)(2,1)S(1)}, u32[]{:S(2)}, u32[]{:S(2)}) collective-permute-start(bf16[5,2,32,128]{3,2,1,0:T(8,128)(2,1)S(1)} %collective-permute-done.6.refs_2_), channel_id=1, source_target_pairs={{0,8},{8,0},{16,24},{24,16},{1,9},{9,1},{17,25},{25,17},{2,10},{10... | collective-permute-start | bytes 245768 | tf_op jit(solution)/shard_map/ppermute | solution.py:316
  22.0 1.0 %copy-start.1 = (bf16[512,512]{1,0:T(8,128)(2,1)S(1)}, bf16[512,512]{1,0:T(8,128)(2,1)}, u32[]{:S(2)}) copy-start(bf16[512,512]{1,0:T(8,128)(2,1)} %factor.1) | copy-start | bytes 1572868
